TPU v7x, 32 devices: a whole 2x2x4 slice. The times are simulated.
32 devices in a mesh: smp: 8 (over z, y), par: 4 (over x, core).
Axes of the slice: x: 2, y: 2, z: 4, core: 2. Of those that a mesh axis runs over, the one named last changes fastest.
Arguments:
- derivatives: bfloat16 [640, 2048], P('smp', 'par'), may hold values from -40 to 40
- epsilon: float32 [640], P('smp'), may hold values from -6 to 6
Outputs:
- gram_tile: float32 [640, 640], P('smp', 'par')
- update: float32 [2048], P('par')
All inputs are finite; a program needn't handle non-finite values.
Results may differ from a plain program's by a relative error of at most 0.003.
Values may be sent and summed in bfloat16 or wider, within the bound.
No kernel may reach another device: no remote copies, remote signals or barrier semaphores. Data moves between devices by JAX's collectives and lax.ppermute only.
A program may use at most 64 MiB of HBM per device.

v0:
```python
import math

import jax
import jax.numpy as jnp
from jax import lax
from jax.sharding import PartitionSpec as P


def shards(derivatives, epsilon):
    total_rows = derivatives.shape[0] * lax.axis_size("smp")
    factor = 1.0 / math.sqrt(total_rows)
    totals = lax.psum(jnp.sum(derivatives.astype(jnp.float32), axis=0), "smp")
    column_mean = totals / total_rows

    def center(values):
        return ((values.astype(jnp.float32) - column_mean) * factor).astype(jnp.bfloat16)

    own_rows = center(derivatives)
    partial_terms = jnp.dot(
        own_rows,
        center(lax.all_gather(derivatives, "smp", axis=0, tiled=True)).T,
        preferred_element_type=jnp.float32,
    )
    gram_tile = lax.psum_scatter(partial_terms, "par", scatter_dimension=1, tiled=True)
    local_sum = jnp.dot(epsilon, own_rows.astype(jnp.float32), precision=lax.Precision.HIGHEST)
    update = lax.psum(local_sum, "smp")
    return (gram_tile, update)


def solution(mesh):
    in_specs = (P("smp", "par"), P("smp"))
    out_specs = (P("smp", "par"), P("par"))
    return jax.shard_map(shards, mesh=mesh, in_specs=in_specs, out_specs=out_specs, check_vma=False)
```

profile of v0, /device:TPU:0, one launch (start us, length us, event | category | flops | bytes accessed | tf_op | source)
XLA Modules:
  0.0 90.6 jit_solution(17457802798909675866)
XLA Ops:
  7.2 0.0 copy-start
  7.2 0.0 copy-start.1
  7.2 0.0 reduce-scatter.4.cloned.1.call-start
  7.2 0.9 %convert_reduce_fusion = f32[512]{0:T(512)S(1)} fusion(bf16[80,512]{1,0:T(8,128)(2,1)} %param.2), kind=kLoop, calls=%fused_computation.5 | loop fusion | flops 81408 | bytes 83968 | tf_op jit(solution)/shard_map/reduce_sum | solution.py:12
  8.2 33.6 %all_gather.3 = bf16[640,512]{1,0:T(8,128)(2,1)S(1)} all-gather(bf16[80,512]{1,0:T(8,128)(2,1)} %param.2), channel_id=1, replica_groups=mesh['smp'=8,'par'=4] {'smp'}, dimensions={0}, use_global_device_ids=true | all-gather | bytes 737280 | tf_op jit(solution)/shard_map/all_gather | solution.py:21
  41.8 21.4 %psum.14 = f32[512]{0:T(512)S(1)} all-reduce(f32[512]{0:T(512)S(1)} %convert_reduce_fusion), channel_id=1, replica_groups=mesh['smp'=8,'par'=4] {'smp'}, use_global_device_ids=true, to_apply=%region_1.0 | all-reduce | flops 512 | bytes 4096 | tf_op jit(solution)/shard_map/psum | solution.py:12
  63.2 0.0 copy-done.1
  63.2 1.1 %convolution_bitcast_fusion = f32[640,80]{1,0:T(8,128)} fusion(bf16[640,512]{1,0:T(8,128)(2,1)S(1)} %all_gather.3, f32[512]{0:T(512)S(1)} %broadcast_multiply_fusion, bf16[80,512]{1,0:T(8,128)(2,1)S(1)} %copy-done.1), kind=kOutput, calls=%fused_computation.1 | convolution fusion | flops 53903360 | bytes 944128
  64.3 0.0 reduce-scatter.4.cloned.1.call-update
  64.3 0.0 copy-done
  64.3 0.2 fusion.4
  64.5 17.7 %psum.15 = f32[512]{0:T(512)} all-reduce(f32[512]{0:T(512)S(1)} %bitcast.8), channel_id=1, replica_groups=mesh['smp'=8,'par'=4] {'smp'}, use_global_device_ids=true, to_apply=%region_3.0 | all-reduce | flops 512 | bytes 4096 | tf_op jit(solution)/shard_map/psum | solution.py:26
  82.2 0.0 reduce-scatter.4.cloned.1.call-done
  82.2 1.6 %copy.5 = f32[80,160]{1,0:T(8,128)} copy(f32[80,160]{0,1:T(8,128)} %bitcast.7) | data formatting | bytes 102400
  (1 shorter events, 0.0 us)
Async XLA Ops:
  7.2 57.2 %copy-start = (f32[80]{0:T(128)S(1)}, f32[80]{0:T(128)}, u32[]{:S(2)}) copy-start(f32[80]{0:T(128)} %param.3) | copy-start | bytes 964
  7.2 56.1 %copy-start.1 = (bf16[80,512]{1,0:T(8,128)(2,1)S(1)}, bf16[80,512]{1,0:T(8,128)(2,1)}, u32[]{:S(2)}) copy-start(bf16[80,512]{1,0:T(8,128)(2,1)} %param.2) | copy-start | bytes 245764
  7.2 75.0 %reduce-scatter.4.cloned.1.call-start = ((), (), s32[]{:S(2)}) async-start(), calls=%async_computation.1 | async-start | bytes 409600
Sparse Core Ops, SparseCore 0:
  64.4 17.6 reduce-scatter.3
where the time goes:
time: 90.9 us; the launch traced here: 90.6 us
  blocking collectives  72.8 us (80%)
  between operations  14.1 us (16%)
  local copies, waits for them, and re-layouts  1.62 us (2%)
  matrix products  1.21 us (1%)
  other arithmetic  0.94 us (1%)
    all_gather x1, blocking collectives, shards(): lax.all_gather(derivatives, 'smp', axis=0, tiled=True)  33.6 us
    psum x1, blocking collectives, shards(): totals = lax.psum(jnp.sum(derivatives.astype(jnp.float32), axis=0), 'smp')  21.4 us
    psum x1, blocking collectives, shards(): update = lax.psum(local_sum, 'smp')  17.7 us
  transfers between devices with their start and end apart: 1, of which 0 were waited for; matrix products, arithmetic and copies ran while one was open for 0% of the time, Pallas kernels for 0%

commit v1 on v0

v1 whole, which is shorter than its diff:
```python
import functools
import math

import jax
import jax.numpy as jnp
from jax import lax
from jax.experimental import pallas as pl
from jax.experimental.pallas import tpu as pltpu
from jax.sharding import PartitionSpec as P


EXTRA = 8
GRANT = 8 << 20
DIRECT = 8


def centered(values, mean, factor):
    return ((values.astype(jnp.float32) - mean) * factor).astype(jnp.bfloat16)


def pack_kernel(rows, derivatives_ref, epsilon_ref, packed_ref):
    packed_ref[:rows, :] = derivatives_ref[...]
    left = epsilon_ref[...]
    packed_ref[rows:, :] = jnp.zeros((EXTRA, packed_ref.shape[1]), jnp.bfloat16)
    parts = []
    for _ in range(3):
        part = left.astype(jnp.bfloat16)
        left = left - part.astype(jnp.float32)
        parts.append(part.astype(jnp.float32))
    parts.append(jnp.zeros((EXTRA - 3, rows), jnp.float32))
    packed_ref[rows:, :rows] = jnp.concatenate(parts, axis=0).astype(jnp.bfloat16)


def pack(derivatives, epsilon):
    rows, columns = derivatives.shape
    return pl.pallas_call(
        functools.partial(pack_kernel, rows),
        out_shape=jax.ShapeDtypeStruct((rows + EXTRA, columns), jnp.bfloat16),
        compiler_params=pltpu.CompilerParams(vmem_limit_bytes=GRANT),
        name="pack",
    )(derivatives, epsilon.reshape(1, rows))


def tile_kernel(n, m, rows, total_rows, *refs):
    blocks, (kept_ref, sent_ref, update_ref, held, sums) = refs[:n], refs[n:]
    me = lax.axis_index("smp")
    mine = lax.axis_index("par")
    per = n // m
    factor = 1.0 / math.sqrt(total_rows)
    for step, block in enumerate(blocks):
        source = jnp.bitwise_xor(me, step)
        sums[pl.ds(source, 1), :] = jnp.sum(block[:rows, :].astype(jnp.float32), axis=0, keepdims=True)
    mean = jnp.sum(sums[...], axis=0, keepdims=True) / total_rows
    own = None
    for step, block in enumerate(blocks):
        terms = centered(block[:rows, :], mean, factor)
        own = terms if step == 0 else own
        source = jnp.bitwise_xor(me, step)
        place = jnp.bitwise_xor(source // per, mine) * per + source % per
        held[pl.ds(pl.multiple_of(place * rows, rows), rows), :] = terms
        update = jnp.dot(block[rows:, :rows], terms, preferred_element_type=jnp.float32)
        sums[pl.ds(source, 1), :] = jnp.sum(update, axis=0, keepdims=True)
    update_ref[...] = jnp.sum(sums[...], axis=0, keepdims=True)
    half = (n // 2) * rows
    contract = (((1,), (1,)), ((), ()))
    sent_ref[...] = lax.dot_general(own, held[half:, :], contract, preferred_element_type=jnp.float32).astype(jnp.bfloat16)
    kept_ref[...] = lax.dot_general(own, held[:half, :], contract, preferred_element_type=jnp.float32)


def tiles(blocks, m, rows, total_rows):
    n, columns = len(blocks), blocks[0].shape[1]
    half = (n // 2) * rows
    return pl.pallas_call(
        functools.partial(tile_kernel, n, m, rows, total_rows),
        out_shape=(
            jax.ShapeDtypeStruct((rows, half), jnp.float32),
            jax.ShapeDtypeStruct((rows, half), jnp.bfloat16),
            jax.ShapeDtypeStruct((1, columns), jnp.float32),
        ),
        scratch_shapes=[pltpu.VMEM((n * rows, columns), jnp.bfloat16), pltpu.VMEM((n, columns), jnp.float32)],
        compiler_params=pltpu.CompilerParams(vmem_limit_bytes=GRANT),
        name="tiles",
    )(*blocks)


def swap(value, axis, bit):
    return lax.ppermute(value, axis, [(i, i ^ bit) for i in range(lax.axis_size(axis))])


ORDER = ((0, 4), (0, 2), (0, 1), (4, 2), (2, 1), (4, 1), (6, 1))


def direct(derivatives, epsilon):
    n, m = lax.axis_size("smp"), lax.axis_size("par")
    rows = derivatives.shape[0]
    blocks = {0: pack(derivatives, epsilon)}
    for source, bit in ORDER:
        blocks[source ^ bit] = swap(blocks[source], "smp", bit)
    kept, sent, update = tiles([blocks[step] for step in range(n)], m, rows, rows * n)
    both = kept + swap(sent, "par", 2).astype(jnp.float32)
    width = rows * n // m
    gram_tile = both[:, :width] + swap(both[:, width:], "par", 1)
    return (gram_tile, update.reshape(-1))


def gathered(derivatives, epsilon):
    total_rows = derivatives.shape[0] * lax.axis_size("smp")
    factor = 1.0 / math.sqrt(total_rows)
    everything = lax.all_gather(derivatives, "smp", axis=0, tiled=True)
    mean = jnp.sum(everything.astype(jnp.float32), axis=0) / total_rows
    own = centered(derivatives, mean, factor)
    partial_terms = jnp.dot(own, centered(everything, mean, factor).T, preferred_element_type=jnp.float32)
    gram_tile = lax.psum_scatter(partial_terms, "par", scatter_dimension=1, tiled=True)
    local_sum = jnp.dot(epsilon, own.astype(jnp.float32), precision=lax.Precision.HIGHEST)
    return (gram_tile, lax.psum(local_sum, "smp"))


def shards(derivatives, epsilon):
    n, m = lax.axis_size("smp"), lax.axis_size("par")
    if n == DIRECT and m == 4:
        return direct(derivatives, epsilon)
    return gathered(derivatives, epsilon)


def solution(mesh):
    in_specs = (P("smp", "par"), P("smp"))
    out_specs = (P("smp", "par"), P("par"))
    return jax.shard_map(shards, mesh=mesh, in_specs=in_specs, out_specs=out_specs, check_vma=False)
```

time: 90.9 us -> 29.3 us (0.32)
  blocking collectives: 72.8 us -> 0 us
  starting transfers between devices: 0.04 us -> 13.5 us
  between operations: 14.1 us -> 0.67 us
  waiting for transfers between devices: 0.02 us -> 11.6 us
  matrix products: 1.21 us -> 0 us
  Pallas kernels: 0 us -> 1.1 us
    psum x2 -> x0, blocking collectives: 39.1 us -> none  [the longest x1 21.4 us: shards(): totals = lax.psum(jnp.sum(derivatives.astype(jnp.float32), axis=0), 'smp')]
    all_gather x1 -> x0, blocking collectives: 33.6 us -> none  [shards(): lax.all_gather(derivatives, 'smp', axis=0, tiled=True)]
    ppermute x0 -> x9, starting transfers between devices: none -> 13.5 us  [swap(): lax.ppermute(value, axis, [(i, i ^ bit) for i in range(lax.axis_size(axis...]
    ppermute x0 -> x9, waiting for transfers between devices: none -> 11.6 us  [swap(): lax.ppermute(value, axis, [(i, i ^ bit) for i in range(lax.axis_size(axis...]
    pallas_call x0 -> x2, Pallas kernels: none -> 1.1 us  [the longest x1 1.08 us: tiles(): pl.pallas_call(functools.partial(tile_kernel, n, m, rows, total_rows), ou...]
    unnamed x1 -> x0, matrix products: 1.05 us -> none
    reduce_sum x1 -> x0, other arithmetic: 0.93 us -> none  [shards(): totals = lax.psum(jnp.sum(derivatives.astype(jnp.float32), axis=0), 'smp')]
  transfers between devices with their start and end apart: 1 -> 9, of which waited for: 0 -> 7; matrix products, arithmetic and copies ran while one was open for 0% -> 0% of each run, Pallas kernels for 0% -> 0%
where the time goes in v1:
time: 29.3 us; the launch traced here: 29.1 us
  starting transfers between devices  13.5 us (46%)
  waiting for transfers between devices  11.6 us (40%)
  local copies, waits for them, and re-layouts  1.61 us (5%)
  Pallas kernels  1.1 us (4%)
  between operations  0.67 us (2%)
  other arithmetic  0.66 us (2%)
    ppermute x9, starting transfers between devices, swap(): lax.ppermute(value, axis, [(i, i ^ bit) for i in range(lax.axis_size(axis...  13.5 us
    ppermute x9, waiting for transfers between devices, swap(): lax.ppermute(value, axis, [(i, i ^ bit) for i in range(lax.axis_size(axis...  11.6 us
    unnamed x4, local copies, waits for them, and re-layouts  1.53 us
    pallas_call x1, Pallas kernels, tiles(): pl.pallas_call(functools.partial(tile_kernel, n, m, rows, total_rows), ou...  1.08 us
    add x1, other arithmetic, direct(): gram_tile = both[:, :width] + swap(both[:, width:], 'par', 1)  0.65 us
  transfers between devices with their start and end apart: 9, of which 7 were waited for; matrix products, arithmetic and copies ran while one was open for 0% of the time, Pallas kernels for 0%

profile of v1, /device:TPU:0, one launch (start us, length us, event | category | flops | bytes accessed | tf_op | source)
XLA Modules:
  0.0 29.1 jit_solution(17370574543822367954)
XLA Ops:
  0.6 0.0 copy-start.1
  0.6 0.6 %copy-done.1 = f32[80]{0:T(128)S(1)} copy-done((f32[80]{0:T(128)S(1)}, f32[80]{0:T(128)}, u32[]{:S(2)}) %copy-start.1) | copy-done | bytes 344
  1.3 0.0 copy-start
  1.3 0.9 %copy-done = bf16[80,512]{1,0:T(8,128)(2,1)S(1)} copy-done((bf16[80,512]{1,0:T(8,128)(2,1)S(1)}, bf16[80,512]{1,0:T(8,128)(2,1)}, u32[]{:S(2)}) %copy-start) | copy-done | bytes 81944
  2.2 4.1 %collective-permute-start.3 = (bf16[88,512]{1,0:T(8,128)(2,1)S(1)}, bf16[88,512]{1,0:T(8,128)(2,1)S(1)}, u32[]{:S(2)}, u32[]{:S(2)}) collective-permute-start(bf16[88,512]{1,0:T(8,128)(2,1)S(1)} %pack.1.refs_0_), channel_id=1, source_target_pairs={{0,16},{4,20},{8,24},{12,28},{16,0},{20,4},{24,8},{28,12},{1,17},{... | collective-permute-start | bytes 270344 | tf_op jit(solution)/shard_map/ppermute | solution.py:87
  6.3 1.6 %collective-permute-start.1 = (bf16[88,512]{1,0:T(8,128)(2,1)S(1)}, bf16[88,512]{1,0:T(8,128)(2,1)S(1)}, u32[]{:S(2)}, u32[]{:S(2)}) collective-permute-start(bf16[88,512]{1,0:T(8,128)(2,1)S(1)} %pack.1.refs_0_), channel_id=1, source_target_pairs={{0,8},{4,12},{8,0},{12,4},{16,24},{20,28},{24,16},{28,20},{1,9},{5... | collective-permute-start | bytes 270344 | tf_op jit(solution)/shard_map/ppermute | solution.py:87
  7.9 2.7 %collective-permute-done.3.refs_4_ = bf16[88,512]{1,0:T(8,128)(2,1)S(1)} collective-permute-done((bf16[88,512]{1,0:T(8,128)(2,1)S(1)}, bf16[88,512]{1,0:T(8,128)(2,1)S(1)}, u32[]{:S(2)}, u32[]{:S(2)}) %collective-permute-start.3) | collective-permute-done | bytes 90144 | tf_op jit(solution)/shard_map/ppermute | solution.py:87
  10.6 1.0 %collective-permute-start.5 = (bf16[88,512]{1,0:T(8,128)(2,1)S(1)}, bf16[88,512]{1,0:T(8,128)(2,1)S(1)}, u32[]{:S(2)}, u32[]{:S(2)}) collective-permute-start(bf16[88,512]{1,0:T(8,128)(2,1)S(1)} %collective-permute-done.3.refs_4_), channel_id=1, source_target_pairs={{0,8},{4,12},{8,0},{12,4},{16,24},{20,28},{24,16},{28,20},{1,9},{5... | collective-permute-start | bytes 270344 | tf_op jit(solution)/shard_map/ppermute | solution.py:87
  11.6 1.5 %collective-permute-start = (bf16[88,512]{1,0:T(8,128)(2,1)S(1)}, bf16[88,512]{1,0:T(8,128)(2,1)S(1)}, u32[]{:S(2)}, u32[]{:S(2)}) collective-permute-start(bf16[88,512]{1,0:T(8,128)(2,1)S(1)} %pack.1.refs_0_), channel_id=1, source_target_pairs={{0,4},{4,0},{8,12},{12,8},{16,20},{20,16},{24,28},{28,24},{1,5},{5... | collective-permute-start | bytes 270344 | tf_op jit(solution)/shard_map/ppermute | solution.py:87
  13.1 0.5 %collective-permute-start.4 = (bf16[88,512]{1,0:T(8,128)(2,1)S(1)}, bf16[88,512]{1,0:T(8,128)(2,1)S(1)}, u32[]{:S(2)}, u32[]{:S(2)}) collective-permute-start(bf16[88,512]{1,0:T(8,128)(2,1)S(1)} %collective-permute-done.3.refs_4_), channel_id=1, source_target_pairs={{0,4},{4,0},{8,12},{12,8},{16,20},{20,16},{24,28},{28,24},{1,5},{5... | collective-permute-start | bytes 270344 | tf_op jit(solution)/shard_map/ppermute | solution.py:87
  13.6 0.0 collective-permute-done.1.refs_2_
  13.6 1.5 %collective-permute-start.2 = (bf16[88,512]{1,0:T(8,128)(2,1)S(1)}, bf16[88,512]{1,0:T(8,128)(2,1)S(1)}, u32[]{:S(2)}, u32[]{:S(2)}) collective-permute-start(bf16[88,512]{1,0:T(8,128)(2,1)S(1)} %collective-permute-done.1.refs_2_), channel_id=1, source_target_pairs={{0,4},{4,0},{8,12},{12,8},{16,20},{20,16},{24,28},{28,24},{1,5},{5... | collective-permute-start | bytes 270344 | tf_op jit(solution)/shard_map/ppermute | solution.py:87
  15.1 0.0 collective-permute-done.5.refs_6_
  15.1 1.7 %collective-permute-start.6 = (bf16[88,512]{1,0:T(8,128)(2,1)S(1)}, bf16[88,512]{1,0:T(8,128)(2,1)S(1)}, u32[]{:S(2)}, u32[]{:S(2)}) collective-permute-start(bf16[88,512]{1,0:T(8,128)(2,1)S(1)} %collective-permute-done.5.refs_6_), channel_id=1, source_target_pairs={{0,4},{4,0},{8,12},{12,8},{16,20},{20,16},{24,28},{28,24},{1,5},{5... | collective-permute-start | bytes 270344 | tf_op jit(solution)/shard_map/ppermute | solution.py:87
  16.8 0.2 collective-permute-done.refs_1_
  17.1 1.9 %collective-permute-done.4.refs_5_ = bf16[88,512]{1,0:T(8,128)(2,1)S(1)} collective-permute-done((bf16[88,512]{1,0:T(8,128)(2,1)S(1)}, bf16[88,512]{1,0:T(8,128)(2,1)S(1)}, u32[]{:S(2)}, u32[]{:S(2)}) %collective-permute-start.4) | collective-permute-done | bytes 90144 | tf_op jit(solution)/shard_map/ppermute | solution.py:87
  19.0 1.7 %collective-permute-done.2.refs_3_ = bf16[88,512]{1,0:T(8,128)(2,1)S(1)} collective-permute-done((bf16[88,512]{1,0:T(8,128)(2,1)S(1)}, bf16[88,512]{1,0:T(8,128)(2,1)S(1)}, u32[]{:S(2)}, u32[]{:S(2)}) %collective-permute-start.2) | collective-permute-done | bytes 90144 | tf_op jit(solution)/shard_map/ppermute | solution.py:87
  20.7 1.0 %collective-permute-done.6.refs_7_ = bf16[88,512]{1,0:T(8,128)(2,1)S(1)} collective-permute-done((bf16[88,512]{1,0:T(8,128)(2,1)S(1)}, bf16[88,512]{1,0:T(8,128)(2,1)S(1)}, u32[]{:S(2)}, u32[]{:S(2)}) %collective-permute-start.6) | collective-permute-done | bytes 90144 | tf_op jit(solution)/shard_map/ppermute | solution.py:87
  21.7 1.1 %tiles.1 = (f32[80,320]{1,0:T(8,128)S(1)}, bf16[80,320]{1,0:T(8,128)(2,1)S(1)}, f32[1,512]{1,0:T(1,128)}) custom-call(bf16[88,512]{1,0:T(8,128)(2,1)S(1)} %pack.1.refs_0_, bf16[88,512]{1,0:T(8,128)(2,1)S(1)} %collective-permute-done.refs_1_, bf16[88,512]{1,0:T(8,128)(2,1)S(1)} %collective-permute-done.1.refs_2_, ...), custom_call_target="tpu_custom_call" | custom-call | tf_op jit(solution)/shard_map/tiles/pallas_call | solution.py:73
  22.8 1.5 %collective-permute-start.7 = (bf16[80,320]{1,0:T(8,128)(2,1)S(1)}, bf16[80,320]{1,0:T(8,128)(2,1)S(1)}, u32[]{:S(2)}, u32[]{:S(2)}) collective-permute-start(bf16[80,320]{1,0:T(8,128)(2,1)S(1)} %get-tuple-element.6), channel_id=1, source_target_pairs={{0,2},{1,3},{2,0},{3,1},{4,6},{5,7},{6,4},{7,5},{8,10},{9,11},{10,... | collective-permute-start | bytes 153608 | tf_op jit(solution)/shard_map/ppermute | solution.py:87
  24.3 2.7 %collective-permute-done.7 = bf16[80,320]{1,0:T(8,128)(2,1)S(1)} collective-permute-done((bf16[80,320]{1,0:T(8,128)(2,1)S(1)}, bf16[80,320]{1,0:T(8,128)(2,1)S(1)}, u32[]{:S(2)}, u32[]{:S(2)}) %collective-permute-start.7) | collective-permute-done | bytes 51232 | tf_op jit(solution)/shard_map/ppermute | solution.py:87
  27.0 0.1 slice.9
  27.1 0.1 collective-permute-start.8
  27.2 1.3 %collective-permute-done.8 = f32[80,160]{1,0:T(8,128)S(1)} collective-permute-done((f32[80,160]{1,0:T(8,128)S(1)}, f32[80,160]{1,0:T(8,128)S(1)}, u32[]{:S(2)}, u32[]{:S(2)}) %collective-permute-start.8) | collective-permute-done | bytes 51232 | tf_op jit(solution)/shard_map/ppermute | solution.py:87
  28.5 0.6 %slice_add_fusion = f32[80,160]{1,0:T(8,128)} fusion(f32[80,160]{1,0:T(8,128)S(1)} %collective-permute-done.8, f32[80,320]{1,0:T(8,128)S(1)} %convert_add_fusion), kind=kLoop, calls=%fused_computation.1 | loop fusion | flops 12800 | bytes 153600 | tf_op jit(solution)/shard_map/add | solution.py:102
  (2 shorter events, 0.0 us)
Async XLA Ops:
  0.6 0.7 %copy-start.1 = (f32[80]{0:T(128)S(1)}, f32[80]{0:T(128)}, u32[]{:S(2)}) copy-start(f32[80]{0:T(128)} %param.3) | copy-start | bytes 964
  1.3 0.9 %copy-start = (bf16[80,512]{1,0:T(8,128)(2,1)S(1)}, bf16[80,512]{1,0:T(8,128)(2,1)}, u32[]{:S(2)}) copy-start(bf16[80,512]{1,0:T(8,128)(2,1)} %derivatives_ref.1) | copy-start | bytes 245764
  2.2 8.4 %collective-permute-start.3 = (bf16[88,512]{1,0:T(8,128)(2,1)S(1)}, bf16[88,512]{1,0:T(8,128)(2,1)S(1)}, u32[]{:S(2)}, u32[]{:S(2)}) collective-permute-start(bf16[88,512]{1,0:T(8,128)(2,1)S(1)} %pack.1.refs_0_), channel_id=1, source_target_pairs={{0,16},{4,20},{8,24},{12,28},{16,0},{20,4},{24,8},{28,12},{1,17},{... | collective-permute-start | bytes 270344 | tf_op jit(solution)/shard_map/ppermute | solution.py:87
  6.3 7.3 %collective-permute-start.1 = (bf16[88,512]{1,0:T(8,128)(2,1)S(1)}, bf16[88,512]{1,0:T(8,128)(2,1)S(1)}, u32[]{:S(2)}, u32[]{:S(2)}) collective-permute-start(bf16[88,512]{1,0:T(8,128)(2,1)S(1)} %pack.1.refs_0_), channel_id=1, source_target_pairs={{0,8},{4,12},{8,0},{12,4},{16,24},{20,28},{24,16},{28,20},{1,9},{5... | collective-permute-start | bytes 270344 | tf_op jit(solution)/shard_map/ppermute | solution.py:87
  10.6 4.5 %collective-permute-start.5 = (bf16[88,512]{1,0:T(8,128)(2,1)S(1)}, bf16[88,512]{1,0:T(8,128)(2,1)S(1)}, u32[]{:S(2)}, u32[]{:S(2)}) collective-permute-start(bf16[88,512]{1,0:T(8,128)(2,1)S(1)} %collective-permute-done.3.refs_4_), channel_id=1, source_target_pairs={{0,8},{4,12},{8,0},{12,4},{16,24},{20,28},{24,16},{28,20},{1,9},{5... | collective-permute-start | bytes 270344 | tf_op jit(solution)/shard_map/ppermute | solution.py:87
  11.6 5.5 %collective-permute-start = (bf16[88,512]{1,0:T(8,128)(2,1)S(1)}, bf16[88,512]{1,0:T(8,128)(2,1)S(1)}, u32[]{:S(2)}, u32[]{:S(2)}) collective-permute-start(bf16[88,512]{1,0:T(8,128)(2,1)S(1)} %pack.1.refs_0_), channel_id=1, source_target_pairs={{0,4},{4,0},{8,12},{12,8},{16,20},{20,16},{24,28},{28,24},{1,5},{5... | collective-permute-start | bytes 270344 | tf_op jit(solution)/shard_map/ppermute | solution.py:87
  13.1 5.9 %collective-permute-start.4 = (bf16[88,512]{1,0:T(8,128)(2,1)S(1)}, bf16[88,512]{1,0:T(8,128)(2,1)S(1)}, u32[]{:S(2)}, u32[]{:S(2)}) collective-permute-start(bf16[88,512]{1,0:T(8,128)(2,1)S(1)} %collective-permute-done.3.refs_4_), channel_id=1, source_target_pairs={{0,4},{4,0},{8,12},{12,8},{16,20},{20,16},{24,28},{28,24},{1,5},{5... | collective-permute-start | bytes 270344 | tf_op jit(solution)/shard_map/ppermute | solution.py:87
  13.6 7.1 %collective-permute-start.2 = (bf16[88,512]{1,0:T(8,128)(2,1)S(1)}, bf16[88,512]{1,0:T(8,128)(2,1)S(1)}, u32[]{:S(2)}, u32[]{:S(2)}) collective-permute-start(bf16[88,512]{1,0:T(8,128)(2,1)S(1)} %collective-permute-done.1.refs_2_), channel_id=1, source_target_pairs={{0,4},{4,0},{8,12},{12,8},{16,20},{20,16},{24,28},{28,24},{1,5},{5... | collective-permute-start | bytes 270344 | tf_op jit(solution)/shard_map/ppermute | solution.py:87
  15.1 6.6 %collective-permute-start.6 = (bf16[88,512]{1,0:T(8,128)(2,1)S(1)}, bf16[88,512]{1,0:T(8,128)(2,1)S(1)}, u32[]{:S(2)}, u32[]{:S(2)}) collective-permute-start(bf16[88,512]{1,0:T(8,128)(2,1)S(1)} %collective-permute-done.5.refs_6_), channel_id=1, source_target_pairs={{0,4},{4,0},{8,12},{12,8},{16,20},{20,16},{24,28},{28,24},{1,5},{5... | collective-permute-start | bytes 270344 | tf_op jit(solution)/shard_map/ppermute | solution.py:87
  22.8 4.2 %collective-permute-start.7 = (bf16[80,320]{1,0:T(8,128)(2,1)S(1)}, bf16[80,320]{1,0:T(8,128)(2,1)S(1)}, u32[]{:S(2)}, u32[]{:S(2)}) collective-permute-start(bf16[80,320]{1,0:T(8,128)(2,1)S(1)} %get-tuple-element.6), channel_id=1, source_target_pairs={{0,2},{1,3},{2,0},{3,1},{4,6},{5,7},{6,4},{7,5},{8,10},{9,11},{10,... | collective-permute-start | bytes 153608 | tf_op jit(solution)/shard_map/ppermute | solution.py:87
  27.1 1.3 %collective-permute-start.8 = (f32[80,160]{1,0:T(8,128)S(1)}, f32[80,160]{1,0:T(8,128)S(1)}, u32[]{:S(2)}, u32[]{:S(2)}) collective-permute-start(f32[80,160]{1,0:T(8,128)S(1)} %slice.9), channel_id=1, source_target_pairs={{0,1},{1,0},{2,3},{3,2},{4,5},{5,4},{6,7},{7,6},{8,9},{9,8},{10,11... | collective-permute-start | bytes 153608 | tf_op jit(solution)/shard_map/ppermute | solution.py:87

commit v2 on v1

v2 whole, which is shorter than its diff:
```python
import functools
import math

import jax
import jax.numpy as jnp
from jax import lax
from jax.experimental import pallas as pl
from jax.experimental.pallas import tpu as pltpu
from jax.sharding import PartitionSpec as P


EXTRA = 8
PARTS = 3
GRANT = 4 << 20
MESSAGES = ((4, (0,)), (2, (0,)), (1, (0,)), (2, (4,)), (1, (2,)), (1, (4,)), (1, (6,)))


def centered(values, mean, factor):
    return ((values.astype(jnp.float32) - mean) * factor).astype(jnp.bfloat16)


def parts_of(value):
    parts = []
    for _ in range(PARTS):
        part = value.astype(jnp.bfloat16).astype(jnp.float32)
        value = value - part
        parts.append(part)
    return parts


def call(kernel, out_shape, scratch=()):
    return pl.pallas_call(
        kernel,
        out_shape=out_shape,
        scratch_shapes=scratch,
        compiler_params=pltpu.CompilerParams(vmem_limit_bytes=GRANT),
    )


def pack_kernel(values_hbm, epsilon_hbm, packed_ref, values, epsilon, arrived):
    rows, columns = values.shape
    copies = [
        pltpu.make_async_copy(source, target, arrived.at[at])
        for at, (source, target) in enumerate(((values_hbm, values), (epsilon_hbm, epsilon)))
    ]
    for copy in copies:
        copy.start()
    for copy in copies:
        copy.wait()
    block = values[...]
    packed_ref[:rows, :] = block
    wide = [jnp.zeros((1, columns - rows), jnp.float32)]
    lines = [jnp.concatenate([part] + wide, axis=1) for part in parts_of(epsilon[...])]
    lines += parts_of(jnp.sum(block.astype(jnp.float32), axis=0, keepdims=True))
    lines.append(jnp.zeros((EXTRA - 2 * PARTS, columns), jnp.float32))
    packed_ref[rows:, :] = jnp.concatenate(lines, axis=0).astype(jnp.bfloat16)


def pack(derivatives, epsilon):
    rows, columns = derivatives.shape
    return pl.pallas_call(
        pack_kernel,
        out_shape=jax.ShapeDtypeStruct((rows + EXTRA, columns), jnp.bfloat16),
        in_specs=[pl.BlockSpec(memory_space=pltpu.HBM)] * 2,
        scratch_shapes=[pltpu.VMEM((rows, columns), jnp.bfloat16), pltpu.VMEM((1, rows), jnp.float32), pltpu.SemaphoreType.DMA((2,))],
        compiler_params=pltpu.CompilerParams(vmem_limit_bytes=GRANT),
        name="pack",
    )(pltpu.with_memory_space_constraint(derivatives, pltpu.HBM), pltpu.with_memory_space_constraint(epsilon.reshape(1, rows), pltpu.HBM))


def join_kernel(packed, places, *refs):
    arrays, joined_ref = refs[:-1], refs[-1]
    for slot, (at, place) in enumerate(places):
        joined_ref[slot * packed : (slot + 1) * packed, :] = arrays[at][place * packed : (place + 1) * packed, :]


def tile_kernel(total_rows, where, *refs):
    count = 1 + max(at for at, _ in where)
    arrays, (kept_ref, sent_ref, update_ref, held, lines) = refs[:count], refs[count:]
    n, _ = lines.shape
    rows = total_rows // n
    packed = rows + EXTRA
    me, mine = lax.axis_index("smp"), lax.axis_index("par")
    factor = 1.0 / math.sqrt(total_rows)
    blocks = [arrays[at].at[packed * slot : packed * (slot + 1), :] for at, slot in where]
    for step, block in enumerate(blocks):
        tail = block[rows:, :].astype(jnp.float32)
        lines[pl.ds(jnp.bitwise_xor(me, step), 1), :] = jnp.sum(tail[PARTS : 2 * PARTS, :], axis=0, keepdims=True)
    mean = jnp.sum(lines[...], axis=0, keepdims=True) / total_rows
    own = None
    for step, block in enumerate(blocks):
        terms = centered(block[:rows, :], mean, factor)
        own = terms if step == 0 else own
        source = jnp.bitwise_xor(me, step)
        place = jnp.bitwise_xor(source // 2, mine) * 2 + source % 2
        held[pl.ds(pl.multiple_of(place * rows, rows), rows), :] = terms
        weighted = jnp.dot(block[rows:, :rows], terms, preferred_element_type=jnp.float32)
        lines[pl.ds(source, 1), :] = jnp.sum(weighted[:PARTS, :], axis=0, keepdims=True)
    half = total_rows // 2
    contract = (((1,), (1,)), ((), ()))
    sent_ref[...] = lax.dot_general(own, held[half:, :], contract, preferred_element_type=jnp.float32).astype(jnp.bfloat16)
    kept_ref[...] = lax.dot_general(own, held[:half, :], contract, preferred_element_type=jnp.float32)
    update_ref[...] = jnp.sum(lines[...], axis=0, keepdims=True)


def swap(value, axis, bit):
    return lax.ppermute(value, axis, [(i, i ^ bit) for i in range(lax.axis_size(axis))])


def direct(derivatives, epsilon):
    n, m = lax.axis_size("smp"), lax.axis_size("par")
    rows, columns = derivatives.shape
    half = rows * n // 2
    height = rows + EXTRA
    arrays, where = [pack(derivatives, epsilon)], {0: (0, 0)}
    for at, (bit, sources) in enumerate(MESSAGES):
        used = sorted({where[source][0] for source in sources})
        value = arrays[used[0]]
        if len(used) > 1 or value.shape[0] != len(sources) * height:
            places = tuple((used.index(where[source][0]), where[source][1]) for source in sources)
            shape = jax.ShapeDtypeStruct((len(sources) * height, columns), jnp.bfloat16)
            value = call(functools.partial(join_kernel, height, places), shape)(*(arrays[one] for one in used))
        arrays.append(swap(value, "smp", bit))
        for slot, source in enumerate(sources):
            where[source ^ bit] = (at + 1, slot)
    kept, sent, update = call(
        functools.partial(tile_kernel, rows * n, tuple(where[step] for step in range(n))),
        (
            jax.ShapeDtypeStruct((rows, half), jnp.float32),
            jax.ShapeDtypeStruct((rows, half), jnp.bfloat16),
            jax.ShapeDtypeStruct((1, columns), jnp.float32),
        ),
        [pltpu.VMEM((n * rows, columns), jnp.bfloat16), pltpu.VMEM((n, columns), jnp.float32)],
    )(*arrays)
    both = kept + swap(sent, "par", 2).astype(jnp.float32)
    width = rows * n // m
    gram_tile = both[:, :width] + swap(both[:, width:], "par", 1)
    return (gram_tile, update.reshape(-1))


def gathered(derivatives, epsilon):
    total_rows = derivatives.shape[0] * lax.axis_size("smp")
    factor = 1.0 / math.sqrt(total_rows)
    everything = lax.all_gather(derivatives, "smp", axis=0, tiled=True)
    mean = jnp.sum(everything.astype(jnp.float32), axis=0) / total_rows
    own = centered(derivatives, mean, factor)
    partial_terms = jnp.dot(own, centered(everything, mean, factor).T, preferred_element_type=jnp.float32)
    gram_tile = lax.psum_scatter(partial_terms, "par", scatter_dimension=1, tiled=True)
    local_sum = jnp.dot(epsilon, own.astype(jnp.float32), precision=lax.Precision.HIGHEST)
    return (gram_tile, lax.psum(local_sum, "smp"))


def solution(mesh):
    in_specs = (P("smp", "par"), P("smp"))
    out_specs = (P("smp", "par"), P("par"))

    def shards(derivatives, epsilon):
        return (direct if small else gathered)(derivatives, epsilon)

    small = (mesh.shape["smp"], mesh.shape["par"]) == (8, 4)
    return jax.shard_map(shards, mesh=mesh, in_specs=in_specs, out_specs=out_specs, check_vma=False)
```

time: 29.3 us -> 28.6 us (0.976)
  local copies, waits for them, and re-layouts: 1.61 us -> 0.08 us
  Pallas kernels: 1.1 us -> 1.94 us
    unnamed x4 -> x0, local copies, waits for them, and re-layouts: 1.53 us -> none
    pallas_call x2, Pallas kernels: 1.1 us -> 1.94 us  [the longest x1 1.01 us: direct(): call(functools.partial(tile_kernel, rows * n, tuple((where[step] for step...]
  transfers between devices with their start and end apart: 9 -> 9, of which waited for: 7 -> 6; matrix products, arithmetic and copies ran while one was open for 0% -> 0% of each run, Pallas kernels for 0% -> 0%
where the time goes in v2:
time: 28.6 us; the launch traced here: 28.4 us
  starting transfers between devices  13.5 us (47%)
  waiting for transfers between devices  11.6 us (41%)
  Pallas kernels  1.94 us (7%)
  between operations  0.67 us (2%)
  other arithmetic  0.66 us (2%)
    ppermute x9, starting transfers between devices, swap(): lax.ppermute(value, axis, [(i, i ^ bit) for i in range(lax.axis_size(axis...  13.5 us
    ppermute x9, waiting for transfers between devices, swap(): lax.ppermute(value, axis, [(i, i ^ bit) for i in range(lax.axis_size(axis...  11.6 us
    pallas_call x1, Pallas kernels, direct(): call(functools.partial(tile_kernel, rows * n, tuple((where[step] for step...  1.01 us
    pallas_call x1, Pallas kernels, pack(): pl.pallas_call(pack_kernel, out_shape=jax.ShapeDtypeStruct((rows + EXTRA,...  0.93 us
    add x1, other arithmetic, direct(): gram_tile = both[:, :width] + swap(both[:, width:], 'par', 1)  0.65 us
  transfers between devices with their start and end apart: 9, of which 6 were waited for; matrix products, arithmetic and copies ran while one was open for 0% of the time, Pallas kernels for 0%

profile of v2, /device:TPU:0, one launch (start us, length us, event | category | flops | bytes accessed | tf_op | source)
XLA Modules:
  0.0 28.4 jit_solution(9661824798352262595)
XLA Ops:
  0.6 0.9 %pack.1.refs_0_ = bf16[88,512]{1,0:T(8,128)(2,1)S(1)} custom-call(bf16[80,512]{1,0:T(8,128)(2,1)} %values_hbm.1, f32[1,80]{1,0:T(1,128)} %bitcast.2), custom_call_target="tpu_custom_call" | custom-call | tf_op jit(solution)/shard_map/pack/pallas_call | solution.py:61
  1.6 4.1 %collective-permute-start = (bf16[88,512]{1,0:T(8,128)(2,1)S(1)}, bf16[88,512]{1,0:T(8,128)(2,1)S(1)}, u32[]{:S(2)}, u32[]{:S(2)}) collective-permute-start(bf16[88,512]{1,0:T(8,128)(2,1)S(1)} %pack.1.refs_0_), channel_id=1, source_target_pairs={{0,16},{4,20},{8,24},{12,28},{16,0},{20,4},{24,8},{28,12},{1,17},{... | collective-permute-start | bytes 270344 | tf_op jit(solution)/shard_map/ppermute | solution.py:107
  5.7 1.6 %collective-permute-start.1 = (bf16[88,512]{1,0:T(8,128)(2,1)S(1)}, bf16[88,512]{1,0:T(8,128)(2,1)S(1)}, u32[]{:S(2)}, u32[]{:S(2)}) collective-permute-start(bf16[88,512]{1,0:T(8,128)(2,1)S(1)} %pack.1.refs_0_), channel_id=1, source_target_pairs={{0,8},{4,12},{8,0},{12,4},{16,24},{20,28},{24,16},{28,20},{1,9},{5... | collective-permute-start | bytes 270344 | tf_op jit(solution)/shard_map/ppermute | solution.py:107
  7.3 2.7 %collective-permute-done.refs_1_ = bf16[88,512]{1,0:T(8,128)(2,1)S(1)} collective-permute-done((bf16[88,512]{1,0:T(8,128)(2,1)S(1)}, bf16[88,512]{1,0:T(8,128)(2,1)S(1)}, u32[]{:S(2)}, u32[]{:S(2)}) %collective-permute-start) | collective-permute-done | bytes 90144 | tf_op jit(solution)/shard_map/ppermute | solution.py:107
  10.0 1.0 %collective-permute-start.3 = (bf16[88,512]{1,0:T(8,128)(2,1)S(1)}, bf16[88,512]{1,0:T(8,128)(2,1)S(1)}, u32[]{:S(2)}, u32[]{:S(2)}) collective-permute-start(bf16[88,512]{1,0:T(8,128)(2,1)S(1)} %collective-permute-done.refs_1_), channel_id=1, source_target_pairs={{0,8},{4,12},{8,0},{12,4},{16,24},{20,28},{24,16},{28,20},{1,9},{5... | collective-permute-start | bytes 270344 | tf_op jit(solution)/shard_map/ppermute | solution.py:107
  11.0 1.5 %collective-permute-start.2 = (bf16[88,512]{1,0:T(8,128)(2,1)S(1)}, bf16[88,512]{1,0:T(8,128)(2,1)S(1)}, u32[]{:S(2)}, u32[]{:S(2)}) collective-permute-start(bf16[88,512]{1,0:T(8,128)(2,1)S(1)} %pack.1.refs_0_), channel_id=1, source_target_pairs={{0,4},{4,0},{8,12},{12,8},{16,20},{20,16},{24,28},{28,24},{1,5},{5... | collective-permute-start | bytes 270344 | tf_op jit(solution)/shard_map/ppermute | solution.py:107
  12.5 0.5 %collective-permute-start.5 = (bf16[88,512]{1,0:T(8,128)(2,1)S(1)}, bf16[88,512]{1,0:T(8,128)(2,1)S(1)}, u32[]{:S(2)}, u32[]{:S(2)}) collective-permute-start(bf16[88,512]{1,0:T(8,128)(2,1)S(1)} %collective-permute-done.refs_1_), channel_id=1, source_target_pairs={{0,4},{4,0},{8,12},{12,8},{16,20},{20,16},{24,28},{28,24},{1,5},{5... | collective-permute-start | bytes 270344 | tf_op jit(solution)/shard_map/ppermute | solution.py:107
  13.0 0.0 collective-permute-done.1.refs_2_
  13.0 1.5 %collective-permute-start.4 = (bf16[88,512]{1,0:T(8,128)(2,1)S(1)}, bf16[88,512]{1,0:T(8,128)(2,1)S(1)}, u32[]{:S(2)}, u32[]{:S(2)}) collective-permute-start(bf16[88,512]{1,0:T(8,128)(2,1)S(1)} %collective-permute-done.1.refs_2_), channel_id=1, source_target_pairs={{0,4},{4,0},{8,12},{12,8},{16,20},{20,16},{24,28},{28,24},{1,5},{5... | collective-permute-start | bytes 270344 | tf_op jit(solution)/shard_map/ppermute | solution.py:107
  14.5 0.0 collective-permute-done.3.refs_4_
  14.5 1.7 %collective-permute-start.6 = (bf16[88,512]{1,0:T(8,128)(2,1)S(1)}, bf16[88,512]{1,0:T(8,128)(2,1)S(1)}, u32[]{:S(2)}, u32[]{:S(2)}) collective-permute-start(bf16[88,512]{1,0:T(8,128)(2,1)S(1)} %collective-permute-done.3.refs_4_), channel_id=1, source_target_pairs={{0,4},{4,0},{8,12},{12,8},{16,20},{20,16},{24,28},{28,24},{1,5},{5... | collective-permute-start | bytes 270344 | tf_op jit(solution)/shard_map/ppermute | solution.py:107
  16.2 0.2 collective-permute-done.2.refs_3_
  16.5 3.7 %collective-permute-done.4.refs_5_ = bf16[88,512]{1,0:T(8,128)(2,1)S(1)} collective-permute-done((bf16[88,512]{1,0:T(8,128)(2,1)S(1)}, bf16[88,512]{1,0:T(8,128)(2,1)S(1)}, u32[]{:S(2)}, u32[]{:S(2)}) %collective-permute-start.4) | collective-permute-done | bytes 90144 | tf_op jit(solution)/shard_map/ppermute | solution.py:107
  20.1 0.0 collective-permute-done.5.refs_6_
  20.1 1.0 %collective-permute-done.6.refs_7_ = bf16[88,512]{1,0:T(8,128)(2,1)S(1)} collective-permute-done((bf16[88,512]{1,0:T(8,128)(2,1)S(1)}, bf16[88,512]{1,0:T(8,128)(2,1)S(1)}, u32[]{:S(2)}, u32[]{:S(2)}) %collective-permute-start.6) | collective-permute-done | bytes 90144 | tf_op jit(solution)/shard_map/ppermute | solution.py:107
  21.1 1.0 %shard_map.41 = (f32[80,320]{1,0:T(8,128)S(1)}, bf16[80,320]{1,0:T(8,128)(2,1)S(1)}, f32[1,512]{1,0:T(1,128)}) custom-call(bf16[88,512]{1,0:T(8,128)(2,1)S(1)} %pack.1.refs_0_, bf16[88,512]{1,0:T(8,128)(2,1)S(1)} %collective-permute-done.refs_1_, bf16[88,512]{1,0:T(8,128)(2,1)S(1)} %collective-permute-done.1.refs_2_, ...), custom_call_target="tpu_custom_call" | custom-call | tf_op jit(solution)/shard_map/pallas_call | solution.py:126
  22.1 1.5 %collective-permute-start.7 = (bf16[80,320]{1,0:T(8,128)(2,1)S(1)}, bf16[80,320]{1,0:T(8,128)(2,1)S(1)}, u32[]{:S(2)}, u32[]{:S(2)}) collective-permute-start(bf16[80,320]{1,0:T(8,128)(2,1)S(1)} %get-tuple-element.6), channel_id=1, source_target_pairs={{0,2},{1,3},{2,0},{3,1},{4,6},{5,7},{6,4},{7,5},{8,10},{9,11},{10,... | collective-permute-start | bytes 153608 | tf_op jit(solution)/shard_map/ppermute | solution.py:107
  23.6 2.7 %collective-permute-done.7 = bf16[80,320]{1,0:T(8,128)(2,1)S(1)} collective-permute-done((bf16[80,320]{1,0:T(8,128)(2,1)S(1)}, bf16[80,320]{1,0:T(8,128)(2,1)S(1)}, u32[]{:S(2)}, u32[]{:S(2)}) %collective-permute-start.7) | collective-permute-done | bytes 51232 | tf_op jit(solution)/shard_map/ppermute | solution.py:107
  26.3 0.1 slice.9
  26.4 0.1 collective-permute-start.8
  26.5 1.3 %collective-permute-done.8 = f32[80,160]{1,0:T(8,128)S(1)} collective-permute-done((f32[80,160]{1,0:T(8,128)S(1)}, f32[80,160]{1,0:T(8,128)S(1)}, u32[]{:S(2)}, u32[]{:S(2)}) %collective-permute-start.8) | collective-permute-done | bytes 51232 | tf_op jit(solution)/shard_map/ppermute | solution.py:107
  27.8 0.6 %slice_add_fusion = f32[80,160]{1,0:T(8,128)} fusion(f32[80,160]{1,0:T(8,128)S(1)} %collective-permute-done.8, f32[80,320]{1,0:T(8,128)S(1)} %convert_add_fusion), kind=kLoop, calls=%fused_computation.1 | loop fusion | flops 12800 | bytes 153600 | tf_op jit(solution)/shard_map/add | solution.py:137
  (1 shorter events, 0.0 us)
Async XLA Ops:
  1.6 8.4 %collective-permute-start = (bf16[88,512]{1,0:T(8,128)(2,1)S(1)}, bf16[88,512]{1,0:T(8,128)(2,1)S(1)}, u32[]{:S(2)}, u32[]{:S(2)}) collective-permute-start(bf16[88,512]{1,0:T(8,128)(2,1)S(1)} %pack.1.refs_0_), channel_id=1, source_target_pairs={{0,16},{4,20},{8,24},{12,28},{16,0},{20,4},{24,8},{28,12},{1,17},{... | collective-permute-start | bytes 270344 | tf_op jit(solution)/shard_map/ppermute | solution.py:107
  5.7 7.3 %collective-permute-start.1 = (bf16[88,512]{1,0:T(8,128)(2,1)S(1)}, bf16[88,512]{1,0:T(8,128)(2,1)S(1)}, u32[]{:S(2)}, u32[]{:S(2)}) collective-permute-start(bf16[88,512]{1,0:T(8,128)(2,1)S(1)} %pack.1.refs_0_), channel_id=1, source_target_pairs={{0,8},{4,12},{8,0},{12,4},{16,24},{20,28},{24,16},{28,20},{1,9},{5... | collective-permute-start | bytes 270344 | tf_op jit(solution)/shard_map/ppermute | solution.py:107
  10.0 4.5 %collective-permute-start.3 = (bf16[88,512]{1,0:T(8,128)(2,1)S(1)}, bf16[88,512]{1,0:T(8,128)(2,1)S(1)}, u32[]{:S(2)}, u32[]{:S(2)}) collective-permute-start(bf16[88,512]{1,0:T(8,128)(2,1)S(1)} %collective-permute-done.refs_1_), channel_id=1, source_target_pairs={{0,8},{4,12},{8,0},{12,4},{16,24},{20,28},{24,16},{28,20},{1,9},{5... | collective-permute-start | bytes 270344 | tf_op jit(solution)/shard_map/ppermute | solution.py:107
  11.0 5.5 %collective-permute-start.2 = (bf16[88,512]{1,0:T(8,128)(2,1)S(1)}, bf16[88,512]{1,0:T(8,128)(2,1)S(1)}, u32[]{:S(2)}, u32[]{:S(2)}) collective-permute-start(bf16[88,512]{1,0:T(8,128)(2,1)S(1)} %pack.1.refs_0_), channel_id=1, source_target_pairs={{0,4},{4,0},{8,12},{12,8},{16,20},{20,16},{24,28},{28,24},{1,5},{5... | collective-permute-start | bytes 270344 | tf_op jit(solution)/shard_map/ppermute | solution.py:107
  12.5 7.6 %collective-permute-start.5 = (bf16[88,512]{1,0:T(8,128)(2,1)S(1)}, bf16[88,512]{1,0:T(8,128)(2,1)S(1)}, u32[]{:S(2)}, u32[]{:S(2)}) collective-permute-start(bf16[88,512]{1,0:T(8,128)(2,1)S(1)} %collective-permute-done.refs_1_), channel_id=1, source_target_pairs={{0,4},{4,0},{8,12},{12,8},{16,20},{20,16},{24,28},{28,24},{1,5},{5... | collective-permute-start | bytes 270344 | tf_op jit(solution)/shard_map/ppermute | solution.py:107
  13.0 7.1 %collective-permute-start.4 = (bf16[88,512]{1,0:T(8,128)(2,1)S(1)}, bf16[88,512]{1,0:T(8,128)(2,1)S(1)}, u32[]{:S(2)}, u32[]{:S(2)}) collective-permute-start(bf16[88,512]{1,0:T(8,128)(2,1)S(1)} %collective-permute-done.1.refs_2_), channel_id=1, source_target_pairs={{0,4},{4,0},{8,12},{12,8},{16,20},{20,16},{24,28},{28,24},{1,5},{5... | collective-permute-start | bytes 270344 | tf_op jit(solution)/shard_map/ppermute | solution.py:107
  14.5 6.6 %collective-permute-start.6 = (bf16[88,512]{1,0:T(8,128)(2,1)S(1)}, bf16[88,512]{1,0:T(8,128)(2,1)S(1)}, u32[]{:S(2)}, u32[]{:S(2)}) collective-permute-start(bf16[88,512]{1,0:T(8,128)(2,1)S(1)} %collective-permute-done.3.refs_4_), channel_id=1, source_target_pairs={{0,4},{4,0},{8,12},{12,8},{16,20},{20,16},{24,28},{28,24},{1,5},{5... | collective-permute-start | bytes 270344 | tf_op jit(solution)/shard_map/ppermute | solution.py:107
  22.1 4.2 %collective-permute-start.7 = (bf16[80,320]{1,0:T(8,128)(2,1)S(1)}, bf16[80,320]{1,0:T(8,128)(2,1)S(1)}, u32[]{:S(2)}, u32[]{:S(2)}) collective-permute-start(bf16[80,320]{1,0:T(8,128)(2,1)S(1)} %get-tuple-element.6), channel_id=1, source_target_pairs={{0,2},{1,3},{2,0},{3,1},{4,6},{5,7},{6,4},{7,5},{8,10},{9,11},{10,... | collective-permute-start | bytes 153608 | tf_op jit(solution)/shard_map/ppermute | solution.py:107
  26.4 1.3 %collective-permute-start.8 = (f32[80,160]{1,0:T(8,128)S(1)}, f32[80,160]{1,0:T(8,128)S(1)}, u32[]{:S(2)}, u32[]{:S(2)}) collective-permute-start(f32[80,160]{1,0:T(8,128)S(1)} %slice.9), channel_id=1, source_target_pairs={{0,1},{1,0},{2,3},{3,2},{4,5},{5,4},{6,7},{7,6},{8,9},{9,8},{10,11... | collective-permute-start | bytes 153608 | tf_op jit(solution)/shard_map/ppermute | solution.py:107

commit v3 on v2

--- a/solution.py
+++ b/solution.py
@@ -74,33 +74,54 @@
         joined_ref[slot * packed : (slot + 1) * packed, :] = arrays[at][place * packed : (place + 1) * packed, :]
 
 
-def tile_kernel(total_rows, where, *refs):
-    count = 1 + max(at for at, _ in where)
-    arrays, (kept_ref, sent_ref, update_ref, held, lines) = refs[:count], refs[count:]
-    n, _ = lines.shape
-    rows = total_rows // n
-    packed = rows + EXTRA
-    me, mine = lax.axis_index("smp"), lax.axis_index("par")
+def source_of(step):
+    return jnp.bitwise_xor(lax.axis_index("smp"), step)
+
+
+def place_of(step, rows):
+    source = source_of(step)
+    apart = jnp.bitwise_xor(source // 2, lax.axis_index("par"))
+    place = apart % 2 * 4 + apart // 2 * 2 + source % 2
+    return pl.ds(pl.multiple_of(place * rows, rows), rows)
+
+
+def product(left, right):
+    return lax.dot_general(left, right, (((1,), (1,)), ((), ())), preferred_element_type=jnp.float32)
+
+
+def blocks_of(where, arrays, packed):
+    return [arrays[at].at[packed * slot : packed * (slot + 1), :] for at, slot in where]
+
+
+def send_kernel(total_rows, where, *refs):
+    arrays, (sent_ref, held_ref, lines) = refs[:-3], refs[-3:]
+    rows = total_rows // len(where)
     factor = 1.0 / math.sqrt(total_rows)
-    blocks = [arrays[at].at[packed * slot : packed * (slot + 1), :] for at, slot in where]
+    blocks = blocks_of(where, arrays, rows + EXTRA)
     for step, block in enumerate(blocks):
         tail = block[rows:, :].astype(jnp.float32)
-        lines[pl.ds(jnp.bitwise_xor(me, step), 1), :] = jnp.sum(tail[PARTS : 2 * PARTS, :], axis=0, keepdims=True)
+        lines[pl.ds(source_of(step), 1), :] = jnp.sum(tail[PARTS : 2 * PARTS, :], axis=0, keepdims=True)
     mean = jnp.sum(lines[...], axis=0, keepdims=True) / total_rows
     own = None
     for step, block in enumerate(blocks):
         terms = centered(block[:rows, :], mean, factor)
         own = terms if step == 0 else own
-        source = jnp.bitwise_xor(me, step)
-        place = jnp.bitwise_xor(source // 2, mine) * 2 + source % 2
-        held[pl.ds(pl.multiple_of(place * rows, rows), rows), :] = terms
+        held_ref[place_of(step, rows), :] = terms
+    for slot in range(2):
+        sent_ref[slot] = product(own, held_ref[(slot + 2) * total_rows // 4 : (slot + 3) * total_rows // 4, :])
+
+
+def keep_kernel(total_rows, where, held_ref, *refs):
+    arrays, (kept_ref, update_ref, lines) = refs[:-3], refs[-3:]
+    rows = total_rows // len(where)
+    for step, block in enumerate(blocks_of(where, arrays, rows + EXTRA)):
+        terms = held_ref[place_of(step, rows), :]
         weighted = jnp.dot(block[rows:, :rows], terms, preferred_element_type=jnp.float32)
-        lines[pl.ds(source, 1), :] = jnp.sum(weighted[:PARTS, :], axis=0, keepdims=True)
-    half = total_rows // 2
-    contract = (((1,), (1,)), ((), ()))
-    sent_ref[...] = lax.dot_general(own, held[half:, :], contract, preferred_element_type=jnp.float32).astype(jnp.bfloat16)
-    kept_ref[...] = lax.dot_general(own, held[:half, :], contract, preferred_element_type=jnp.float32)
+        lines[pl.ds(source_of(step), 1), :] = jnp.sum(weighted[:PARTS, :], axis=0, keepdims=True)
     update_ref[...] = jnp.sum(lines[...], axis=0, keepdims=True)
+    own = held_ref[place_of(0, rows), :]
+    for slot in range(2):
+        kept_ref[slot] = product(own, held_ref[slot * total_rows // 4 : (slot + 1) * total_rows // 4, :])
 
 
 def swap(value, axis, bit):
@@ -110,7 +131,6 @@
 def direct(derivatives, epsilon):
     n, m = lax.axis_size("smp"), lax.axis_size("par")
     rows, columns = derivatives.shape
-    half = rows * n // 2
     height = rows + EXTRA
     arrays, where = [pack(derivatives, epsilon)], {0: (0, 0)}
     for at, (bit, sources) in enumerate(MESSAGES):
@@ -123,18 +143,20 @@
         arrays.append(swap(value, "smp", bit))
         for slot, source in enumerate(sources):
             where[source ^ bit] = (at + 1, slot)
-    kept, sent, update = call(
-        functools.partial(tile_kernel, rows * n, tuple(where[step] for step in range(n))),
-        (
-            jax.ShapeDtypeStruct((rows, half), jnp.float32),
-            jax.ShapeDtypeStruct((rows, half), jnp.bfloat16),
-            jax.ShapeDtypeStruct((1, columns), jnp.float32),
-        ),
-        [pltpu.VMEM((n * rows, columns), jnp.bfloat16), pltpu.VMEM((n, columns), jnp.float32)],
+    where = tuple(where[step] for step in range(n))
+    lines = [pltpu.VMEM((n, columns), jnp.float32)]
+    tile = jax.ShapeDtypeStruct((2, rows, rows * n // m), jnp.float32)
+    sent, held = call(
+        functools.partial(send_kernel, rows * n, where),
+        (tile, jax.ShapeDtypeStruct((n * rows, columns), jnp.bfloat16)),
+        lines,
     )(*arrays)
-    both = kept + swap(sent, "par", 2).astype(jnp.float32)
-    width = rows * n // m
-    gram_tile = both[:, :width] + swap(both[:, width:], "par", 1)
+    got = swap(sent, "par", 1)
+    kept, update = call(
+        functools.partial(keep_kernel, rows * n, where), (tile, jax.ShapeDtypeStruct((1, columns), jnp.float32)), lines
+    )(held, *arrays)
+    both = kept + got
+    gram_tile = both[0] + swap(both[1].astype(jnp.bfloat16), "par", 2).astype(jnp.float32)
     return (gram_tile, update.reshape(-1))
 
 

time: 28.6 us -> 27.9 us (0.976)
  waiting for transfers between devices: 11.6 us -> 10.6 us
  Pallas kernels: 1.94 us -> 2.3 us
    ppermute x9, waiting for transfers between devices: 11.6 us -> 10.6 us  [swap(): lax.ppermute(value, axis, [(i, i ^ bit) for i in range(lax.axis_size(axis...]
    pallas_call x1 -> x2, Pallas kernels: 1.01 us -> 1.37 us  [the longest x1 0.88 us: direct(): call(functools.partial(keep_kernel, rows * n, where), (tile, jax.ShapeDty...]
  transfers between devices with their start and end apart: 9 -> 9, of which waited for: 6 -> 6; matrix products, arithmetic and copies ran while one was open for 0% -> 0% of each run, Pallas kernels for 0% -> 3%
where the time goes in v3:
time: 27.9 us; the launch traced here: 27.8 us
  starting transfers between devices  13.6 us (49%)
  waiting for transfers between devices  10.6 us (38%)
  Pallas kernels  2.3 us (8%)
  between operations  0.67 us (2%)
  other arithmetic  0.66 us (2%)
    ppermute x9, starting transfers between devices, swap(): lax.ppermute(value, axis, [(i, i ^ bit) for i in range(lax.axis_size(axis...  13.6 us
    ppermute x9, waiting for transfers between devices, swap(): lax.ppermute(value, axis, [(i, i ^ bit) for i in range(lax.axis_size(axis...  10.6 us
    pallas_call x1, Pallas kernels, pack(): pl.pallas_call(pack_kernel, out_shape=jax.ShapeDtypeStruct((rows + EXTRA,...  0.93 us
    pallas_call x1, Pallas kernels, direct(): call(functools.partial(keep_kernel, rows * n, where), (tile, jax.ShapeDty...  0.88 us
    add x1, other arithmetic, direct(): both[0] + swap(both[1].astype(jnp.bfloat16), 'par', 2).astype(jnp.float32)  0.64 us
  transfers between devices with their start and end apart: 9, of which 6 were waited for; matrix products, arithmetic and copies ran while one was open for 0% of the time, Pallas kernels for 3%

profile of v3, /device:TPU:0, one launch (start us, length us, event | category | flops | bytes accessed | tf_op | source)
XLA Modules:
  0.0 27.8 jit_solution(17227386199527646473)
XLA Ops:
  0.6 0.9 %pack.1.refs_0_ = bf16[88,512]{1,0:T(8,128)(2,1)S(1)} custom-call(bf16[80,512]{1,0:T(8,128)(2,1)} %values_hbm.1, f32[1,80]{1,0:T(1,128)} %bitcast.8), custom_call_target="tpu_custom_call" | custom-call | tf_op jit(solution)/shard_map/pack/pallas_call | solution.py:61
  1.6 4.1 %collective-permute-start = (bf16[88,512]{1,0:T(8,128)(2,1)S(1)}, bf16[88,512]{1,0:T(8,128)(2,1)S(1)}, u32[]{:S(2)}, u32[]{:S(2)}) collective-permute-start(bf16[88,512]{1,0:T(8,128)(2,1)S(1)} %pack.1.refs_0_), channel_id=1, source_target_pairs={{0,16},{4,20},{8,24},{12,28},{16,0},{20,4},{24,8},{28,12},{1,17},{... | collective-permute-start | bytes 270344 | tf_op jit(solution)/shard_map/ppermute | solution.py:128
  5.7 1.6 %collective-permute-start.1 = (bf16[88,512]{1,0:T(8,128)(2,1)S(1)}, bf16[88,512]{1,0:T(8,128)(2,1)S(1)}, u32[]{:S(2)}, u32[]{:S(2)}) collective-permute-start(bf16[88,512]{1,0:T(8,128)(2,1)S(1)} %pack.1.refs_0_), channel_id=1, source_target_pairs={{0,8},{4,12},{8,0},{12,4},{16,24},{20,28},{24,16},{28,20},{1,9},{5... | collective-permute-start | bytes 270344 | tf_op jit(solution)/shard_map/ppermute | solution.py:128
  7.3 2.7 %collective-permute-done.refs_1_ = bf16[88,512]{1,0:T(8,128)(2,1)S(1)} collective-permute-done((bf16[88,512]{1,0:T(8,128)(2,1)S(1)}, bf16[88,512]{1,0:T(8,128)(2,1)S(1)}, u32[]{:S(2)}, u32[]{:S(2)}) %collective-permute-start) | collective-permute-done | bytes 90144 | tf_op jit(solution)/shard_map/ppermute | solution.py:128
  10.0 1.0 %collective-permute-start.3 = (bf16[88,512]{1,0:T(8,128)(2,1)S(1)}, bf16[88,512]{1,0:T(8,128)(2,1)S(1)}, u32[]{:S(2)}, u32[]{:S(2)}) collective-permute-start(bf16[88,512]{1,0:T(8,128)(2,1)S(1)} %collective-permute-done.refs_1_), channel_id=1, source_target_pairs={{0,8},{4,12},{8,0},{12,4},{16,24},{20,28},{24,16},{28,20},{1,9},{5... | collective-permute-start | bytes 270344 | tf_op jit(solution)/shard_map/ppermute | solution.py:128
  11.0 1.5 %collective-permute-start.2 = (bf16[88,512]{1,0:T(8,128)(2,1)S(1)}, bf16[88,512]{1,0:T(8,128)(2,1)S(1)}, u32[]{:S(2)}, u32[]{:S(2)}) collective-permute-start(bf16[88,512]{1,0:T(8,128)(2,1)S(1)} %pack.1.refs_0_), channel_id=1, source_target_pairs={{0,4},{4,0},{8,12},{12,8},{16,20},{20,16},{24,28},{28,24},{1,5},{5... | collective-permute-start | bytes 270344 | tf_op jit(solution)/shard_map/ppermute | solution.py:128
  12.5 0.5 %collective-permute-start.5 = (bf16[88,512]{1,0:T(8,128)(2,1)S(1)}, bf16[88,512]{1,0:T(8,128)(2,1)S(1)}, u32[]{:S(2)}, u32[]{:S(2)}) collective-permute-start(bf16[88,512]{1,0:T(8,128)(2,1)S(1)} %collective-permute-done.refs_1_), channel_id=1, source_target_pairs={{0,4},{4,0},{8,12},{12,8},{16,20},{20,16},{24,28},{28,24},{1,5},{5... | collective-permute-start | bytes 270344 | tf_op jit(solution)/shard_map/ppermute | solution.py:128
  13.0 0.0 collective-permute-done.1.refs_2_
  13.0 1.5 %collective-permute-start.4 = (bf16[88,512]{1,0:T(8,128)(2,1)S(1)}, bf16[88,512]{1,0:T(8,128)(2,1)S(1)}, u32[]{:S(2)}, u32[]{:S(2)}) collective-permute-start(bf16[88,512]{1,0:T(8,128)(2,1)S(1)} %collective-permute-done.1.refs_2_), channel_id=1, source_target_pairs={{0,4},{4,0},{8,12},{12,8},{16,20},{20,16},{24,28},{28,24},{1,5},{5... | collective-permute-start | bytes 270344 | tf_op jit(solution)/shard_map/ppermute | solution.py:128
  14.5 0.0 collective-permute-done.3.refs_4_
  14.5 1.7 %collective-permute-start.6 = (bf16[88,512]{1,0:T(8,128)(2,1)S(1)}, bf16[88,512]{1,0:T(8,128)(2,1)S(1)}, u32[]{:S(2)}, u32[]{:S(2)}) collective-permute-start(bf16[88,512]{1,0:T(8,128)(2,1)S(1)} %collective-permute-done.3.refs_4_), channel_id=1, source_target_pairs={{0,4},{4,0},{8,12},{12,8},{16,20},{20,16},{24,28},{28,24},{1,5},{5... | collective-permute-start | bytes 270344 | tf_op jit(solution)/shard_map/ppermute | solution.py:128
  16.2 0.2 collective-permute-done.2.refs_3_
  16.5 3.7 %collective-permute-done.4.refs_5_ = bf16[88,512]{1,0:T(8,128)(2,1)S(1)} collective-permute-done((bf16[88,512]{1,0:T(8,128)(2,1)S(1)}, bf16[88,512]{1,0:T(8,128)(2,1)S(1)}, u32[]{:S(2)}, u32[]{:S(2)}) %collective-permute-start.4) | collective-permute-done | bytes 90144 | tf_op jit(solution)/shard_map/ppermute | solution.py:128
  20.1 0.0 collective-permute-done.5.refs_6_
  20.1 1.0 %collective-permute-done.6.refs_7_ = bf16[88,512]{1,0:T(8,128)(2,1)S(1)} collective-permute-done((bf16[88,512]{1,0:T(8,128)(2,1)S(1)}, bf16[88,512]{1,0:T(8,128)(2,1)S(1)}, u32[]{:S(2)}, u32[]{:S(2)}) %collective-permute-start.6) | collective-permute-done | bytes 90144 | tf_op jit(solution)/shard_map/ppermute | solution.py:128
  21.1 0.5 %shard_map.41 = (f32[2,80,160]{2,1,0:T(8,128)S(1)}, bf16[640,512]{1,0:T(8,128)(2,1)S(1)}) custom-call(bf16[88,512]{1,0:T(8,128)(2,1)S(1)} %pack.1.refs_0_, bf16[88,512]{1,0:T(8,128)(2,1)S(1)} %collective-permute-done.refs_1_, bf16[88,512]{1,0:T(8,128)(2,1)S(1)} %collective-permute-done.1.refs_2_, bf16[88,512]{1,0:T(8,128)(2,1)S(1)} %collective-permute-done.2.refs_3_, ...), custom_call_target="tpu_custom_call" | custom-call | tf_op jit(solution)/shard_map/pallas_call | solution.py:149
  21.6 0.1 collective-permute-start.7
  21.7 0.9 %shard_map.42 = (f32[2,80,160]{2,1,0:T(8,128)S(1)}, f32[1,512]{1,0:T(1,128)}) custom-call(bf16[640,512]{1,0:T(8,128)(2,1)S(1)} %get-tuple-element.6.held_ref, bf16[88,512]{1,0:T(8,128)(2,1)S(1)} %pack.1.refs_0_, bf16[88,512]{1,0:T(8,128)(2,1)S(1)} %collective-permute-done.refs_1_, bf16[88,512]{1,0:T(8,128)(2,1)S(1)} %collective-permute-done.1.refs_2_, ...), custom_call_target="tpu_custom_call" | custom-call | tf_op jit(solution)/shard_map/pallas_call | solution.py:155
  22.5 0.5 %collective-permute-done.7 = f32[2,80,160]{2,1,0:T(8,128)S(1)} collective-permute-done((f32[2,80,160]{2,1,0:T(8,128)S(1)}, f32[2,80,160]{2,1,0:T(8,128)S(1)}, u32[]{:S(2)}, u32[]{:S(2)}) %collective-permute-start.7) | collective-permute-done | bytes 102432 | tf_op jit(solution)/shard_map/ppermute | solution.py:128
  23.1 1.6 %collective-permute-start.8 = (bf16[80,160]{1,0:T(8,128)(2,1)S(1)}, bf16[80,160]{1,0:T(8,128)(2,1)S(1)}, u32[]{:S(2)}, u32[]{:S(2)}) collective-permute-start(bf16[80,160]{1,0:T(8,128)(2,1)S(1)} %fusion.1), channel_id=1, source_target_pairs={{0,2},{1,3},{2,0},{3,1},{4,6},{5,7},{6,4},{7,5},{8,10},{9,11},{10,... | collective-permute-start | bytes 76808 | tf_op jit(solution)/shard_map/ppermute | solution.py:128
  24.6 2.5 %collective-permute-done.8 = bf16[80,160]{1,0:T(8,128)(2,1)S(1)} collective-permute-done((bf16[80,160]{1,0:T(8,128)(2,1)S(1)}, bf16[80,160]{1,0:T(8,128)(2,1)S(1)}, u32[]{:S(2)}, u32[]{:S(2)}) %collective-permute-start.8) | collective-permute-done | bytes 25632 | tf_op jit(solution)/shard_map/ppermute | solution.py:128
  27.1 0.6 %fusion = f32[80,160]{1,0:T(8,128)} fusion(f32[2,80,160]{2,1,0:T(8,128)S(1)} %add.6, bf16[80,160]{1,0:T(8,128)(2,1)S(1)} %collective-permute-done.8), kind=kLoop, calls=%fused_computation.2 | loop fusion | flops 25600 | bytes 128000 | tf_op jit(solution)/shard_map/add | solution.py:159
  (2 shorter events, 0.0 us)
Async XLA Ops:
  1.6 8.4 %collective-permute-start = (bf16[88,512]{1,0:T(8,128)(2,1)S(1)}, bf16[88,512]{1,0:T(8,128)(2,1)S(1)}, u32[]{:S(2)}, u32[]{:S(2)}) collective-permute-start(bf16[88,512]{1,0:T(8,128)(2,1)S(1)} %pack.1.refs_0_), channel_id=1, source_target_pairs={{0,16},{4,20},{8,24},{12,28},{16,0},{20,4},{24,8},{28,12},{1,17},{... | collective-permute-start | bytes 270344 | tf_op jit(solution)/shard_map/ppermute | solution.py:128
  5.7 7.3 %collective-permute-start.1 = (bf16[88,512]{1,0:T(8,128)(2,1)S(1)}, bf16[88,512]{1,0:T(8,128)(2,1)S(1)}, u32[]{:S(2)}, u32[]{:S(2)}) collective-permute-start(bf16[88,512]{1,0:T(8,128)(2,1)S(1)} %pack.1.refs_0_), channel_id=1, source_target_pairs={{0,8},{4,12},{8,0},{12,4},{16,24},{20,28},{24,16},{28,20},{1,9},{5... | collective-permute-start | bytes 270344 | tf_op jit(solution)/shard_map/ppermute | solution.py:128
  10.0 4.5 %collective-permute-start.3 = (bf16[88,512]{1,0:T(8,128)(2,1)S(1)}, bf16[88,512]{1,0:T(8,128)(2,1)S(1)}, u32[]{:S(2)}, u32[]{:S(2)}) collective-permute-start(bf16[88,512]{1,0:T(8,128)(2,1)S(1)} %collective-permute-done.refs_1_), channel_id=1, source_target_pairs={{0,8},{4,12},{8,0},{12,4},{16,24},{20,28},{24,16},{28,20},{1,9},{5... | collective-permute-start | bytes 270344 | tf_op jit(solution)/shard_map/ppermute | solution.py:128
  11.0 5.5 %collective-permute-start.2 = (bf16[88,512]{1,0:T(8,128)(2,1)S(1)}, bf16[88,512]{1,0:T(8,128)(2,1)S(1)}, u32[]{:S(2)}, u32[]{:S(2)}) collective-permute-start(bf16[88,512]{1,0:T(8,128)(2,1)S(1)} %pack.1.refs_0_), channel_id=1, source_target_pairs={{0,4},{4,0},{8,12},{12,8},{16,20},{20,16},{24,28},{28,24},{1,5},{5... | collective-permute-start | bytes 270344 | tf_op jit(solution)/shard_map/ppermute | solution.py:128
  12.5 7.6 %collective-permute-start.5 = (bf16[88,512]{1,0:T(8,128)(2,1)S(1)}, bf16[88,512]{1,0:T(8,128)(2,1)S(1)}, u32[]{:S(2)}, u32[]{:S(2)}) collective-permute-start(bf16[88,512]{1,0:T(8,128)(2,1)S(1)} %collective-permute-done.refs_1_), channel_id=1, source_target_pairs={{0,4},{4,0},{8,12},{12,8},{16,20},{20,16},{24,28},{28,24},{1,5},{5... | collective-permute-start | bytes 270344 | tf_op jit(solution)/shard_map/ppermute | solution.py:128
  13.0 7.1 %collective-permute-start.4 = (bf16[88,512]{1,0:T(8,128)(2,1)S(1)}, bf16[88,512]{1,0:T(8,128)(2,1)S(1)}, u32[]{:S(2)}, u32[]{:S(2)}) collective-permute-start(bf16[88,512]{1,0:T(8,128)(2,1)S(1)} %collective-permute-done.1.refs_2_), channel_id=1, source_target_pairs={{0,4},{4,0},{8,12},{12,8},{16,20},{20,16},{24,28},{28,24},{1,5},{5... | collective-permute-start | bytes 270344 | tf_op jit(solution)/shard_map/ppermute | solution.py:128
  14.5 6.6 %collective-permute-start.6 = (bf16[88,512]{1,0:T(8,128)(2,1)S(1)}, bf16[88,512]{1,0:T(8,128)(2,1)S(1)}, u32[]{:S(2)}, u32[]{:S(2)}) collective-permute-start(bf16[88,512]{1,0:T(8,128)(2,1)S(1)} %collective-permute-done.3.refs_4_), channel_id=1, source_target_pairs={{0,4},{4,0},{8,12},{12,8},{16,20},{20,16},{24,28},{28,24},{1,5},{5... | collective-permute-start | bytes 270344 | tf_op jit(solution)/shard_map/ppermute | solution.py:128
  21.6 1.5 %collective-permute-start.7 = (f32[2,80,160]{2,1,0:T(8,128)S(1)}, f32[2,80,160]{2,1,0:T(8,128)S(1)}, u32[]{:S(2)}, u32[]{:S(2)}) collective-permute-start(f32[2,80,160]{2,1,0:T(8,128)S(1)} %get-tuple-element.8), channel_id=1, source_target_pairs={{0,1},{1,0},{2,3},{3,2},{4,5},{5,4},{6,7},{7,6},{8,9},{9,8},{10,11... | collective-permute-start | bytes 307208 | tf_op jit(solution)/shard_map/ppermute | solution.py:128
  23.1 4.1 %collective-permute-start.8 = (bf16[80,160]{1,0:T(8,128)(2,1)S(1)}, bf16[80,160]{1,0:T(8,128)(2,1)S(1)}, u32[]{:S(2)}, u32[]{:S(2)}) collective-permute-start(bf16[80,160]{1,0:T(8,128)(2,1)S(1)} %fusion.1), channel_id=1, source_target_pairs={{0,2},{1,3},{2,0},{3,1},{4,6},{5,7},{6,4},{7,5},{8,10},{9,11},{10,... | collective-permute-start | bytes 76808 | tf_op jit(solution)/shard_map/ppermute | solution.py:128

commit v4 on v3

--- a/solution.py
+++ b/solution.py
@@ -12,7 +12,8 @@
 EXTRA = 8
 PARTS = 3
 GRANT = 4 << 20
-MESSAGES = ((4, (0,)), (2, (0,)), (1, (0,)), (2, (4,)), (1, (2,)), (1, (4,)), (1, (6,)))
+LANES = 128
+SPARE = 8
 
 
 def centered(values, mean, factor):
@@ -68,10 +69,10 @@
     )(pltpu.with_memory_space_constraint(derivatives, pltpu.HBM), pltpu.with_memory_space_constraint(epsilon.reshape(1, rows), pltpu.HBM))
 
 
-def join_kernel(packed, places, *refs):
-    arrays, joined_ref = refs[:-1], refs[-1]
-    for slot, (at, place) in enumerate(places):
-        joined_ref[slot * packed : (slot + 1) * packed, :] = arrays[at][place * packed : (place + 1) * packed, :]
+def tails_kernel(*refs):
+    for slot, ref in enumerate(refs[:-1]):
+        tail = ref[ref.shape[0] - EXTRA :, : refs[-1].shape[1]]
+        refs[-1][slot * EXTRA : (slot + 1) * EXTRA, :] = tail
 
 
 def source_of(step):
@@ -89,19 +90,17 @@
     return lax.dot_general(left, right, (((1,), (1,)), ((), ())), preferred_element_type=jnp.float32)
 
 
-def blocks_of(where, arrays, packed):
-    return [arrays[at].at[packed * slot : packed * (slot + 1), :] for at, slot in where]
-
-
-def send_kernel(total_rows, where, *refs):
-    arrays, (sent_ref, held_ref, lines) = refs[:-3], refs[-3:]
-    rows = total_rows // len(where)
+def send_kernel(total_rows, *refs):
+    blocks, (sent_ref, held_ref, lines) = refs[:-3], refs[-3:]
+    rows = total_rows // len(blocks)
     factor = 1.0 / math.sqrt(total_rows)
-    blocks = blocks_of(where, arrays, rows + EXTRA)
     for step, block in enumerate(blocks):
-        tail = block[rows:, :].astype(jnp.float32)
-        lines[pl.ds(source_of(step), 1), :] = jnp.sum(tail[PARTS : 2 * PARTS, :], axis=0, keepdims=True)
-    mean = jnp.sum(lines[...], axis=0, keepdims=True) / total_rows
+        if block.shape[0] > rows:
+            line = jnp.sum(block[rows:, :].astype(jnp.float32)[PARTS : 2 * PARTS, :], axis=0, keepdims=True)
+        else:
+            line = jnp.sum(block[...].astype(jnp.float32), axis=0, keepdims=True)
+        lines[pl.ds(source_of(step), 1), :] = line
+    mean = jnp.sum(lines[: len(blocks), :], axis=0, keepdims=True) / total_rows
     own = None
     for step, block in enumerate(blocks):
         terms = centered(block[:rows, :], mean, factor)
@@ -111,17 +110,21 @@
         sent_ref[slot] = product(own, held_ref[(slot + 2) * total_rows // 4 : (slot + 3) * total_rows // 4, :])
 
 
-def keep_kernel(total_rows, where, held_ref, *refs):
-    arrays, (kept_ref, update_ref, lines) = refs[:-3], refs[-3:]
-    rows = total_rows // len(where)
-    for step, block in enumerate(blocks_of(where, arrays, rows + EXTRA)):
-        terms = held_ref[place_of(step, rows), :]
-        weighted = jnp.dot(block[rows:, :rows], terms, preferred_element_type=jnp.float32)
-        lines[pl.ds(source_of(step), 1), :] = jnp.sum(weighted[:PARTS, :], axis=0, keepdims=True)
-    update_ref[...] = jnp.sum(lines[...], axis=0, keepdims=True)
+def keep_kernel(rows, held_ref, kept_ref):
     own = held_ref[place_of(0, rows), :]
     for slot in range(2):
-        kept_ref[slot] = product(own, held_ref[slot * total_rows // 4 : (slot + 1) * total_rows // 4, :])
+        span = held_ref.shape[0] // 4
+        kept_ref[slot] = product(own, held_ref[slot * span : (slot + 1) * span, :])
+
+
+def update_kernel(rows, held_ref, near_ref, far_ref, update_ref, lines):
+    count = held_ref.shape[0] // rows
+    for step in range(count):
+        ref, slot = (near_ref, step) if step < 4 else (far_ref, step - 4)
+        weights = ref[slot * EXTRA : (slot + 1) * EXTRA, :rows]
+        weighted = jnp.dot(weights, held_ref[place_of(step, rows), :], preferred_element_type=jnp.float32)
+        lines[pl.ds(source_of(step), 1), :] = jnp.sum(weighted[:PARTS, :], axis=0, keepdims=True)
+    update_ref[...] = jnp.sum(lines[:count, :], axis=0, keepdims=True)
 
 
 def swap(value, axis, bit):
@@ -131,30 +134,26 @@
 def direct(derivatives, epsilon):
     n, m = lax.axis_size("smp"), lax.axis_size("par")
     rows, columns = derivatives.shape
-    height = rows + EXTRA
-    arrays, where = [pack(derivatives, epsilon)], {0: (0, 0)}
-    for at, (bit, sources) in enumerate(MESSAGES):
-        used = sorted({where[source][0] for source in sources})
-        value = arrays[used[0]]
-        if len(used) > 1 or value.shape[0] != len(sources) * height:
-            places = tuple((used.index(where[source][0]), where[source][1]) for source in sources)
-            shape = jax.ShapeDtypeStruct((len(sources) * height, columns), jnp.bfloat16)
-            value = call(functools.partial(join_kernel, height, places), shape)(*(arrays[one] for one in used))
-        arrays.append(swap(value, "smp", bit))
-        for slot, source in enumerate(sources):
-            where[source ^ bit] = (at + 1, slot)
-    where = tuple(where[step] for step in range(n))
-    lines = [pltpu.VMEM((n, columns), jnp.float32)]
+    far = swap(derivatives, "smp", 4)
+    own = pack(derivatives, epsilon)
+    beside = swap(own, "smp", 2)
+    other = swap(own, "smp", 1)
+    far_beside = swap(far, "smp", 2)
+    beside_other = swap(other, "smp", 2)
+    far_other = swap(far, "smp", 1)
+    far_beside_other = swap(far_beside, "smp", 1)
+    near = (own, other, beside, beside_other)
+    tails = call(tails_kernel, jax.ShapeDtypeStruct((len(near) * EXTRA, LANES), jnp.bfloat16))(*near)
+    far_tails = swap(tails, "smp", 4)
     tile = jax.ShapeDtypeStruct((2, rows, rows * n // m), jnp.float32)
+    lines = [pltpu.VMEM((n + SPARE, columns), jnp.float32)]
     sent, held = call(
-        functools.partial(send_kernel, rows * n, where),
-        (tile, jax.ShapeDtypeStruct((n * rows, columns), jnp.bfloat16)),
-        lines,
-    )(*arrays)
+        functools.partial(send_kernel, rows * n), (tile, jax.ShapeDtypeStruct((n * rows, columns), jnp.bfloat16)), lines
+    )(*near, far, far_other, far_beside, far_beside_other)
     got = swap(sent, "par", 1)
-    kept, update = call(
-        functools.partial(keep_kernel, rows * n, where), (tile, jax.ShapeDtypeStruct((1, columns), jnp.float32)), lines
-    )(held, *arrays)
+    kept = call(functools.partial(keep_kernel, rows), tile)(held)
+    line = jax.ShapeDtypeStruct((1, columns), jnp.float32)
+    update = call(functools.partial(update_kernel, rows), line, lines)(held, tails, far_tails)
     both = kept + got
     gram_tile = both[0] + swap(both[1].astype(jnp.bfloat16), "par", 2).astype(jnp.float32)
     return (gram_tile, update.reshape(-1))

time: 27.9 us -> 28.9 us (1.036)
  starting transfers between devices: 13.6 us -> 15.8 us
  waiting for transfers between devices: 10.6 us -> 9.07 us
    ppermute x9 -> x10, starting transfers between devices: 13.6 us -> 15.8 us  [swap(): lax.ppermute(value, axis, [(i, i ^ bit) for i in range(lax.axis_size(axis...]
    ppermute x9 -> x10, waiting for transfers between devices: 10.6 us -> 9.07 us  [swap(): lax.ppermute(value, axis, [(i, i ^ bit) for i in range(lax.axis_size(axis...]
    pallas_call x2 -> x4, Pallas kernels: 1.37 us -> 1.59 us  [the longest x1 0.82 us: direct(): call(functools.partial(update_kernel, rows), line, lines)]
  transfers between devices with their start and end apart: 9 -> 10, of which waited for: 6 -> 7; matrix products, arithmetic and copies ran while one was open for 0% -> 0% of each run, Pallas kernels for 3% -> 7%
where the time goes in v4:
time: 28.9 us; the launch traced here: 28.7 us
  starting transfers between devices  15.8 us (55%)
  waiting for transfers between devices  9.07 us (31%)
  Pallas kernels  2.56 us (9%)
  other arithmetic  0.67 us (2%)
  between operations  0.67 us (2%)
    ppermute x10, starting transfers between devices, swap(): lax.ppermute(value, axis, [(i, i ^ bit) for i in range(lax.axis_size(axis...  15.8 us
    ppermute x10, waiting for transfers between devices, swap(): lax.ppermute(value, axis, [(i, i ^ bit) for i in range(lax.axis_size(axis...  9.07 us
    pallas_call x1, Pallas kernels, pack(): pl.pallas_call(pack_kernel, out_shape=jax.ShapeDtypeStruct((rows + EXTRA,...  0.97 us
    pallas_call x1, Pallas kernels, direct(): call(functools.partial(update_kernel, rows), line, lines)  0.82 us
    add x1, other arithmetic, direct(): both[0] + swap(both[1].astype(jnp.bfloat16), 'par', 2).astype(jnp.float32)  0.64 us
  transfers between devices with their start and end apart: 10, of which 7 were waited for; matrix products, arithmetic and copies ran while one was open for 0% of the time, Pallas kernels for 7%

profile of v4, /device:TPU:0, one launch (start us, length us, event | category | flops | bytes accessed | tf_op | source)
XLA Modules:
  0.0 28.7 jit_solution(4971271856929212979)
XLA Ops:
  0.6 4.1 %collective-permute-start.3 = (bf16[80,512]{1,0:T(8,128)(2,1)}, bf16[80,512]{1,0:T(8,128)(2,1)S(1)}, u32[]{:S(2)}, u32[]{:S(2)}) collective-permute-start(bf16[80,512]{1,0:T(8,128)(2,1)} %values_hbm.1), channel_id=1, source_target_pairs={{0,16},{4,20},{8,24},{12,28},{16,0},{20,4},{24,8},{28,12},{1,17},{... | collective-permute-start | bytes 245768 | tf_op jit(solution)/shard_map/ppermute | solution.py:131
  4.8 1.0 %pack.1.refs_0_ = bf16[88,512]{1,0:T(8,128)(2,1)S(1)} custom-call(bf16[80,512]{1,0:T(8,128)(2,1)} %values_hbm.1, f32[1,80]{1,0:T(1,128)} %bitcast.9), custom_call_target="tpu_custom_call" | custom-call | tf_op jit(solution)/shard_map/pack/pallas_call | solution.py:62
  5.7 1.6 %collective-permute-start = (bf16[88,512]{1,0:T(8,128)(2,1)S(1)}, bf16[88,512]{1,0:T(8,128)(2,1)S(1)}, u32[]{:S(2)}, u32[]{:S(2)}) collective-permute-start(bf16[88,512]{1,0:T(8,128)(2,1)S(1)} %pack.1.refs_0_), channel_id=1, source_target_pairs={{0,4},{4,0},{8,12},{12,8},{16,20},{20,16},{24,28},{28,24},{1,5},{5... | collective-permute-start | bytes 270344 | tf_op jit(solution)/shard_map/ppermute | solution.py:131
  7.3 1.9 %collective-permute-done.3.refs_4_ = bf16[80,512]{1,0:T(8,128)(2,1)S(1)} collective-permute-done((bf16[80,512]{1,0:T(8,128)(2,1)}, bf16[80,512]{1,0:T(8,128)(2,1)S(1)}, u32[]{:S(2)}, u32[]{:S(2)}) %collective-permute-start.3) | collective-permute-done | bytes 81952 | tf_op jit(solution)/shard_map/ppermute | solution.py:131
  9.2 0.8 %collective-permute-start.5 = (bf16[80,512]{1,0:T(8,128)(2,1)S(1)}, bf16[80,512]{1,0:T(8,128)(2,1)S(1)}, u32[]{:S(2)}, u32[]{:S(2)}) collective-permute-start(bf16[80,512]{1,0:T(8,128)(2,1)S(1)} %collective-permute-done.3.refs_4_), channel_id=1, source_target_pairs={{0,8},{4,12},{8,0},{12,4},{16,24},{20,28},{24,16},{28,20},{1,9},{5... | collective-permute-start | bytes 245768 | tf_op jit(solution)/shard_map/ppermute | solution.py:131
  10.0 1.2 %collective-permute-start.1 = (bf16[88,512]{1,0:T(8,128)(2,1)S(1)}, bf16[88,512]{1,0:T(8,128)(2,1)S(1)}, u32[]{:S(2)}, u32[]{:S(2)}) collective-permute-start(bf16[88,512]{1,0:T(8,128)(2,1)S(1)} %pack.1.refs_0_), channel_id=1, source_target_pairs={{0,8},{4,12},{8,0},{12,4},{16,24},{20,28},{24,16},{28,20},{1,9},{5... | collective-permute-start | bytes 270344 | tf_op jit(solution)/shard_map/ppermute | solution.py:131
  11.2 0.0 collective-permute-done.refs_1_
  11.2 0.8 %collective-permute-start.2 = (bf16[88,512]{1,0:T(8,128)(2,1)S(1)}, bf16[88,512]{1,0:T(8,128)(2,1)S(1)}, u32[]{:S(2)}, u32[]{:S(2)}) collective-permute-start(bf16[88,512]{1,0:T(8,128)(2,1)S(1)} %collective-permute-done.refs_1_), channel_id=1, source_target_pairs={{0,8},{4,12},{8,0},{12,4},{16,24},{20,28},{24,16},{28,20},{1,9},{5... | collective-permute-start | bytes 270344 | tf_op jit(solution)/shard_map/ppermute | solution.py:131
  12.0 1.5 %collective-permute-start.4 = (bf16[80,512]{1,0:T(8,128)(2,1)S(1)}, bf16[80,512]{1,0:T(8,128)(2,1)S(1)}, u32[]{:S(2)}, u32[]{:S(2)}) collective-permute-start(bf16[80,512]{1,0:T(8,128)(2,1)S(1)} %collective-permute-done.3.refs_4_), channel_id=1, source_target_pairs={{0,4},{4,0},{8,12},{12,8},{16,20},{20,16},{24,28},{28,24},{1,5},{5... | collective-permute-start | bytes 245768 | tf_op jit(solution)/shard_map/ppermute | solution.py:131
  13.5 0.9 %collective-permute-done.5.refs_6_ = bf16[80,512]{1,0:T(8,128)(2,1)S(1)} collective-permute-done((bf16[80,512]{1,0:T(8,128)(2,1)S(1)}, bf16[80,512]{1,0:T(8,128)(2,1)S(1)}, u32[]{:S(2)}, u32[]{:S(2)}) %collective-permute-start.5) | collective-permute-done | bytes 81952 | tf_op jit(solution)/shard_map/ppermute | solution.py:131
  14.5 1.7 %collective-permute-start.6 = (bf16[80,512]{1,0:T(8,128)(2,1)S(1)}, bf16[80,512]{1,0:T(8,128)(2,1)S(1)}, u32[]{:S(2)}, u32[]{:S(2)}) collective-permute-start(bf16[80,512]{1,0:T(8,128)(2,1)S(1)} %collective-permute-done.5.refs_6_), channel_id=1, source_target_pairs={{0,4},{4,0},{8,12},{12,8},{16,20},{20,16},{24,28},{28,24},{1,5},{5... | collective-permute-start | bytes 245768 | tf_op jit(solution)/shard_map/ppermute | solution.py:131
  16.2 0.0 collective-permute-done.1.refs_2_
  16.2 0.4 %collective-permute-done.4.refs_5_ = bf16[80,512]{1,0:T(8,128)(2,1)S(1)} collective-permute-done((bf16[80,512]{1,0:T(8,128)(2,1)S(1)}, bf16[80,512]{1,0:T(8,128)(2,1)S(1)}, u32[]{:S(2)}, u32[]{:S(2)}) %collective-permute-start.4) | collective-permute-done | bytes 81952 | tf_op jit(solution)/shard_map/ppermute | solution.py:131
  16.6 0.3 collective-permute-done.2.refs_3_
  16.9 2.0 %collective-permute-done.6.refs_7_ = bf16[80,512]{1,0:T(8,128)(2,1)S(1)} collective-permute-done((bf16[80,512]{1,0:T(8,128)(2,1)S(1)}, bf16[80,512]{1,0:T(8,128)(2,1)S(1)}, u32[]{:S(2)}, u32[]{:S(2)}) %collective-permute-start.6) | collective-permute-done | bytes 81952 | tf_op jit(solution)/shard_map/ppermute | solution.py:131
  18.9 0.5 %shard_map.41 = (f32[2,80,160]{2,1,0:T(8,128)S(1)}, bf16[640,512]{1,0:T(8,128)(2,1)S(1)}) custom-call(bf16[88,512]{1,0:T(8,128)(2,1)S(1)} %pack.1.refs_0_, bf16[88,512]{1,0:T(8,128)(2,1)S(1)} %collective-permute-done.refs_1_, bf16[88,512]{1,0:T(8,128)(2,1)S(1)} %collective-permute-done.1.refs_2_, bf16[88,512]{1,0:T(8,128)(2,1)S(1)} %collective-permute-done.2.refs_3_, ...), custom_call_target="tpu_custom_call" | custom-call | tf_op jit(solution)/shard_map/pallas_call | solution.py:150
  19.5 0.1 collective-permute-start.7
  19.5 0.2 shard_map.42
  19.8 1.1 %collective-permute-done.7 = f32[2,80,160]{2,1,0:T(8,128)S(1)} collective-permute-done((f32[2,80,160]{2,1,0:T(8,128)S(1)}, f32[2,80,160]{2,1,0:T(8,128)S(1)}, u32[]{:S(2)}, u32[]{:S(2)}) %collective-permute-start.7) | collective-permute-done | bytes 102432 | tf_op jit(solution)/shard_map/ppermute | solution.py:131
  21.0 1.7 %collective-permute-start.8 = (bf16[80,160]{1,0:T(8,128)(2,1)S(1)}, bf16[80,160]{1,0:T(8,128)(2,1)S(1)}, u32[]{:S(2)}, u32[]{:S(2)}) collective-permute-start(bf16[80,160]{1,0:T(8,128)(2,1)S(1)} %fusion.1), channel_id=1, source_target_pairs={{0,2},{1,3},{2,0},{3,1},{4,6},{5,7},{6,4},{7,5},{8,10},{9,11},{10,... | collective-permute-start | bytes 76808 | tf_op jit(solution)/shard_map/ppermute | solution.py:131
  22.7 2.2 %collective-permute-start.9 = (bf16[32,128]{1,0:T(8,128)(2,1)S(1)}, bf16[32,128]{1,0:T(8,128)(2,1)S(1)}, u32[]{:S(2)}, u32[]{:S(2)}) collective-permute-start(bf16[32,128]{1,0:T(8,128)(2,1)S(1)} %shard_map.43.near_ref), channel_id=1, source_target_pairs={{0,16},{4,20},{8,24},{12,28},{16,0},{20,4},{24,8},{28,12},{1,17},{... | collective-permute-start | bytes 24584 | tf_op jit(solution)/shard_map/ppermute | solution.py:131
  24.9 2.4 %collective-permute-done.9.far_ref = bf16[32,128]{1,0:T(8,128)(2,1)S(1)} collective-permute-done((bf16[32,128]{1,0:T(8,128)(2,1)S(1)}, bf16[32,128]{1,0:T(8,128)(2,1)S(1)}, u32[]{:S(2)}, u32[]{:S(2)}) %collective-permute-start.9) | collective-permute-done | bytes 8224 | tf_op jit(solution)/shard_map/ppermute | solution.py:131
  27.3 0.8 %shard_map.44 = f32[1,512]{1,0:T(1,128)} custom-call(bf16[640,512]{1,0:T(8,128)(2,1)S(1)} %get-tuple-element.4.held_ref, bf16[32,128]{1,0:T(8,128)(2,1)S(1)} %shard_map.43.near_ref, bf16[32,128]{1,0:T(8,128)(2,1)S(1)} %collective-permute-done.9.far_ref), custom_call_target="tpu_custom_call" | custom-call | tf_op jit(solution)/shard_map/pallas_call | solution.py:156
  28.1 0.0 collective-permute-done.8
  28.1 0.6 %fusion = f32[80,160]{1,0:T(8,128)} fusion(f32[2,80,160]{2,1,0:T(8,128)S(1)} %add.6, bf16[80,160]{1,0:T(8,128)(2,1)S(1)} %collective-permute-done.8), kind=kLoop, calls=%fused_computation.2 | loop fusion | flops 25600 | bytes 128000 | tf_op jit(solution)/shard_map/add | solution.py:158
  (3 shorter events, 0.0 us)
Async XLA Ops:
  0.6 8.5 %collective-permute-start.3 = (bf16[80,512]{1,0:T(8,128)(2,1)}, bf16[80,512]{1,0:T(8,128)(2,1)S(1)}, u32[]{:S(2)}, u32[]{:S(2)}) collective-permute-start(bf16[80,512]{1,0:T(8,128)(2,1)} %values_hbm.1), channel_id=1, source_target_pairs={{0,16},{4,20},{8,24},{12,28},{16,0},{20,4},{24,8},{28,12},{1,17},{... | collective-permute-start | bytes 245768 | tf_op jit(solution)/shard_map/ppermute | solution.py:131
  5.7 5.5 %collective-permute-start = (bf16[88,512]{1,0:T(8,128)(2,1)S(1)}, bf16[88,512]{1,0:T(8,128)(2,1)S(1)}, u32[]{:S(2)}, u32[]{:S(2)}) collective-permute-start(bf16[88,512]{1,0:T(8,128)(2,1)S(1)} %pack.1.refs_0_), channel_id=1, source_target_pairs={{0,4},{4,0},{8,12},{12,8},{16,20},{20,16},{24,28},{28,24},{1,5},{5... | collective-permute-start | bytes 270344 | tf_op jit(solution)/shard_map/ppermute | solution.py:131
  9.2 5.3 %collective-permute-start.5 = (bf16[80,512]{1,0:T(8,128)(2,1)S(1)}, bf16[80,512]{1,0:T(8,128)(2,1)S(1)}, u32[]{:S(2)}, u32[]{:S(2)}) collective-permute-start(bf16[80,512]{1,0:T(8,128)(2,1)S(1)} %collective-permute-done.3.refs_4_), channel_id=1, source_target_pairs={{0,8},{4,12},{8,0},{12,4},{16,24},{20,28},{24,16},{28,20},{1,9},{5... | collective-permute-start | bytes 245768 | tf_op jit(solution)/shard_map/ppermute | solution.py:131
  10.0 6.2 %collective-permute-start.1 = (bf16[88,512]{1,0:T(8,128)(2,1)S(1)}, bf16[88,512]{1,0:T(8,128)(2,1)S(1)}, u32[]{:S(2)}, u32[]{:S(2)}) collective-permute-start(bf16[88,512]{1,0:T(8,128)(2,1)S(1)} %pack.1.refs_0_), channel_id=1, source_target_pairs={{0,8},{4,12},{8,0},{12,4},{16,24},{20,28},{24,16},{28,20},{1,9},{5... | collective-permute-start | bytes 270344 | tf_op jit(solution)/shard_map/ppermute | solution.py:131
  11.2 5.7 %collective-permute-start.2 = (bf16[88,512]{1,0:T(8,128)(2,1)S(1)}, bf16[88,512]{1,0:T(8,128)(2,1)S(1)}, u32[]{:S(2)}, u32[]{:S(2)}) collective-permute-start(bf16[88,512]{1,0:T(8,128)(2,1)S(1)} %collective-permute-done.refs_1_), channel_id=1, source_target_pairs={{0,8},{4,12},{8,0},{12,4},{16,24},{20,28},{24,16},{28,20},{1,9},{5... | collective-permute-start | bytes 270344 | tf_op jit(solution)/shard_map/ppermute | solution.py:131
  12.0 4.6 %collective-permute-start.4 = (bf16[80,512]{1,0:T(8,128)(2,1)S(1)}, bf16[80,512]{1,0:T(8,128)(2,1)S(1)}, u32[]{:S(2)}, u32[]{:S(2)}) collective-permute-start(bf16[80,512]{1,0:T(8,128)(2,1)S(1)} %collective-permute-done.3.refs_4_), channel_id=1, source_target_pairs={{0,4},{4,0},{8,12},{12,8},{16,20},{20,16},{24,28},{28,24},{1,5},{5... | collective-permute-start | bytes 245768 | tf_op jit(solution)/shard_map/ppermute | solution.py:131
  14.5 4.4 %collective-permute-start.6 = (bf16[80,512]{1,0:T(8,128)(2,1)S(1)}, bf16[80,512]{1,0:T(8,128)(2,1)S(1)}, u32[]{:S(2)}, u32[]{:S(2)}) collective-permute-start(bf16[80,512]{1,0:T(8,128)(2,1)S(1)} %collective-permute-done.5.refs_6_), channel_id=1, source_target_pairs={{0,4},{4,0},{8,12},{12,8},{16,20},{20,16},{24,28},{28,24},{1,5},{5... | collective-permute-start | bytes 245768 | tf_op jit(solution)/shard_map/ppermute | solution.py:131
  19.5 1.5 %collective-permute-start.7 = (f32[2,80,160]{2,1,0:T(8,128)S(1)}, f32[2,80,160]{2,1,0:T(8,128)S(1)}, u32[]{:S(2)}, u32[]{:S(2)}) collective-permute-start(f32[2,80,160]{2,1,0:T(8,128)S(1)} %get-tuple-element.5), channel_id=1, source_target_pairs={{0,1},{1,0},{2,3},{3,2},{4,5},{5,4},{6,7},{7,6},{8,9},{9,8},{10,11... | collective-permute-start | bytes 307208 | tf_op jit(solution)/shard_map/ppermute | solution.py:131
  21.0 7.1 %collective-permute-start.8 = (bf16[80,160]{1,0:T(8,128)(2,1)S(1)}, bf16[80,160]{1,0:T(8,128)(2,1)S(1)}, u32[]{:S(2)}, u32[]{:S(2)}) collective-permute-start(bf16[80,160]{1,0:T(8,128)(2,1)S(1)} %fusion.1), channel_id=1, source_target_pairs={{0,2},{1,3},{2,0},{3,1},{4,6},{5,7},{6,4},{7,5},{8,10},{9,11},{10,... | collective-permute-start | bytes 76808 | tf_op jit(solution)/shard_map/ppermute | solution.py:131
  22.7 4.5 %collective-permute-start.9 = (bf16[32,128]{1,0:T(8,128)(2,1)S(1)}, bf16[32,128]{1,0:T(8,128)(2,1)S(1)}, u32[]{:S(2)}, u32[]{:S(2)}) collective-permute-start(bf16[32,128]{1,0:T(8,128)(2,1)S(1)} %shard_map.43.near_ref), channel_id=1, source_target_pairs={{0,16},{4,20},{8,24},{12,28},{16,0},{20,4},{24,8},{28,12},{1,17},{... | collective-permute-start | bytes 24584 | tf_op jit(solution)/shard_map/ppermute | solution.py:131

commit v5 on v4

--- a/solution.py
+++ b/solution.py
@@ -13,6 +13,7 @@
 PARTS = 3
 GRANT = 4 << 20
 LANES = 128
+GROUP = 24
 SPARE = 8
 
 
@@ -125,6 +126,25 @@
         weighted = jnp.dot(weights, held_ref[place_of(step, rows), :], preferred_element_type=jnp.float32)
         lines[pl.ds(source_of(step), 1), :] = jnp.sum(weighted[:PARTS, :], axis=0, keepdims=True)
     update_ref[...] = jnp.sum(lines[:count, :], axis=0, keepdims=True)
+
+
+def middle_kernel(kept_ref, got_ref, base_ref, packed_ref):
+    base_ref[...] = kept_ref[0] + got_ref[0]
+    tile = kept_ref[1] + got_ref[1]
+    rows, width = tile.shape
+    packed_ref[:rows, :] = tile[:, :LANES].astype(jnp.bfloat16)
+    rest = jnp.concatenate([tile[:, LANES:], jnp.zeros((4 * GROUP - rows, width - LANES), jnp.float32)], axis=0)
+    pieces = [rest[at * GROUP : (at + 1) * GROUP, :] for at in range(4)]
+    packed_ref[rows:, :] = jnp.concatenate(pieces, axis=1).astype(jnp.bfloat16)
+
+
+def last_kernel(base_ref, packed_ref, tile_ref):
+    rows, width = base_ref.shape
+    side = width - LANES
+    tile_ref[:, :LANES] = base_ref[:, :LANES] + packed_ref[:rows, :].astype(jnp.float32)
+    rest = packed_ref[rows:, :].astype(jnp.float32)
+    pieces = [rest[:, at * side : (at + 1) * side] for at in range(4)]
+    tile_ref[:, LANES:] = base_ref[:, LANES:] + jnp.concatenate(pieces, axis=0)[:rows, :]
 
 
 def swap(value, axis, bit):
@@ -154,8 +174,12 @@
     kept = call(functools.partial(keep_kernel, rows), tile)(held)
     line = jax.ShapeDtypeStruct((1, columns), jnp.float32)
     update = call(functools.partial(update_kernel, rows), line, lines)(held, tails, far_tails)
-    both = kept + got
-    gram_tile = both[0] + swap(both[1].astype(jnp.bfloat16), "par", 2).astype(jnp.float32)
+    packed_rows = rows + GROUP
+    base, packed = call(
+        middle_kernel,
+        (jax.ShapeDtypeStruct(tile.shape[1:], jnp.float32), jax.ShapeDtypeStruct((packed_rows, LANES), jnp.bfloat16)),
+    )(kept, got)
+    gram_tile = call(last_kernel, jax.ShapeDtypeStruct(tile.shape[1:], jnp.float32))(base, swap(packed, "par", 2))
     return (gram_tile, update.reshape(-1))
 
 

time: 28.9 us -> 28.9 us (level)
  Pallas kernels: 2.56 us -> 3.34 us
  other arithmetic: 0.67 us -> 0 us
    pallas_call x0 -> x2, Pallas kernels: none -> 0.79 us  [the longest x1 0.71 us: direct(): call(last_kernel, jax.ShapeDtypeStruct(tile.shape[1:], jnp.float32))]
    add x2 -> x0, other arithmetic: 0.67 us -> none  [the longest x1 0.64 us: direct(): both[0] + swap(both[1].astype(jnp.bfloat16), 'par', 2).astype(jnp.float32)]
where the time goes in v5:
time: 28.9 us; the launch traced here: 28.8 us
  starting transfers between devices  15.7 us (54%)
  waiting for transfers between devices  9.07 us (31%)
  Pallas kernels  3.34 us (12%)
  between operations  0.66 us (2%)
    ppermute x10, starting transfers between devices, swap(): lax.ppermute(value, axis, [(i, i ^ bit) for i in range(lax.axis_size(axis...  15.7 us
    ppermute x10, waiting for transfers between devices, swap(): lax.ppermute(value, axis, [(i, i ^ bit) for i in range(lax.axis_size(axis...  9.07 us
    pallas_call x1, Pallas kernels, pack(): pl.pallas_call(pack_kernel, out_shape=jax.ShapeDtypeStruct((rows + EXTRA,...  0.97 us
    pallas_call x1, Pallas kernels, direct(): call(functools.partial(update_kernel, rows), line, lines)  0.82 us
    pallas_call x1, Pallas kernels, direct(): call(last_kernel, jax.ShapeDtypeStruct(tile.shape[1:], jnp.float32))  0.71 us
  transfers between devices with their start and end apart: 10, of which 7 were waited for; matrix products, arithmetic and copies ran while one was open for 0% of the time, Pallas kernels for 7%

profile of v5, /device:TPU:0, one launch (start us, length us, event | category | flops | bytes accessed | tf_op | source)
XLA Modules:
  0.0 28.8 jit_solution(3430522056924855857)
XLA Ops:
  0.6 4.1 %collective-permute-start.3 = (bf16[80,512]{1,0:T(8,128)(2,1)}, bf16[80,512]{1,0:T(8,128)(2,1)S(1)}, u32[]{:S(2)}, u32[]{:S(2)}) collective-permute-start(bf16[80,512]{1,0:T(8,128)(2,1)} %values_hbm.1), channel_id=1, source_target_pairs={{0,16},{4,20},{8,24},{12,28},{16,0},{20,4},{24,8},{28,12},{1,17},{... | collective-permute-start | bytes 245768 | tf_op jit(solution)/shard_map/ppermute | solution.py:151
  4.8 1.0 %pack.1.refs_0_ = bf16[88,512]{1,0:T(8,128)(2,1)S(1)} custom-call(bf16[80,512]{1,0:T(8,128)(2,1)} %values_hbm.1, f32[1,80]{1,0:T(1,128)} %bitcast.3), custom_call_target="tpu_custom_call" | custom-call | tf_op jit(solution)/shard_map/pack/pallas_call | solution.py:63
  5.7 1.6 %collective-permute-start = (bf16[88,512]{1,0:T(8,128)(2,1)S(1)}, bf16[88,512]{1,0:T(8,128)(2,1)S(1)}, u32[]{:S(2)}, u32[]{:S(2)}) collective-permute-start(bf16[88,512]{1,0:T(8,128)(2,1)S(1)} %pack.1.refs_0_), channel_id=1, source_target_pairs={{0,4},{4,0},{8,12},{12,8},{16,20},{20,16},{24,28},{28,24},{1,5},{5... | collective-permute-start | bytes 270344 | tf_op jit(solution)/shard_map/ppermute | solution.py:151
  7.3 1.9 %collective-permute-done.3.refs_4_ = bf16[80,512]{1,0:T(8,128)(2,1)S(1)} collective-permute-done((bf16[80,512]{1,0:T(8,128)(2,1)}, bf16[80,512]{1,0:T(8,128)(2,1)S(1)}, u32[]{:S(2)}, u32[]{:S(2)}) %collective-permute-start.3) | collective-permute-done | bytes 81952 | tf_op jit(solution)/shard_map/ppermute | solution.py:151
  9.2 0.8 %collective-permute-start.5 = (bf16[80,512]{1,0:T(8,128)(2,1)S(1)}, bf16[80,512]{1,0:T(8,128)(2,1)S(1)}, u32[]{:S(2)}, u32[]{:S(2)}) collective-permute-start(bf16[80,512]{1,0:T(8,128)(2,1)S(1)} %collective-permute-done.3.refs_4_), channel_id=1, source_target_pairs={{0,8},{4,12},{8,0},{12,4},{16,24},{20,28},{24,16},{28,20},{1,9},{5... | collective-permute-start | bytes 245768 | tf_op jit(solution)/shard_map/ppermute | solution.py:151
  10.0 1.2 %collective-permute-start.1 = (bf16[88,512]{1,0:T(8,128)(2,1)S(1)}, bf16[88,512]{1,0:T(8,128)(2,1)S(1)}, u32[]{:S(2)}, u32[]{:S(2)}) collective-permute-start(bf16[88,512]{1,0:T(8,128)(2,1)S(1)} %pack.1.refs_0_), channel_id=1, source_target_pairs={{0,8},{4,12},{8,0},{12,4},{16,24},{20,28},{24,16},{28,20},{1,9},{5... | collective-permute-start | bytes 270344 | tf_op jit(solution)/shard_map/ppermute | solution.py:151
  11.2 0.0 collective-permute-done.refs_1_
  11.2 0.8 %collective-permute-start.2 = (bf16[88,512]{1,0:T(8,128)(2,1)S(1)}, bf16[88,512]{1,0:T(8,128)(2,1)S(1)}, u32[]{:S(2)}, u32[]{:S(2)}) collective-permute-start(bf16[88,512]{1,0:T(8,128)(2,1)S(1)} %collective-permute-done.refs_1_), channel_id=1, source_target_pairs={{0,8},{4,12},{8,0},{12,4},{16,24},{20,28},{24,16},{28,20},{1,9},{5... | collective-permute-start | bytes 270344 | tf_op jit(solution)/shard_map/ppermute | solution.py:151
  12.0 1.5 %collective-permute-start.4 = (bf16[80,512]{1,0:T(8,128)(2,1)S(1)}, bf16[80,512]{1,0:T(8,128)(2,1)S(1)}, u32[]{:S(2)}, u32[]{:S(2)}) collective-permute-start(bf16[80,512]{1,0:T(8,128)(2,1)S(1)} %collective-permute-done.3.refs_4_), channel_id=1, source_target_pairs={{0,4},{4,0},{8,12},{12,8},{16,20},{20,16},{24,28},{28,24},{1,5},{5... | collective-permute-start | bytes 245768 | tf_op jit(solution)/shard_map/ppermute | solution.py:151
  13.5 0.9 %collective-permute-done.5.refs_6_ = bf16[80,512]{1,0:T(8,128)(2,1)S(1)} collective-permute-done((bf16[80,512]{1,0:T(8,128)(2,1)S(1)}, bf16[80,512]{1,0:T(8,128)(2,1)S(1)}, u32[]{:S(2)}, u32[]{:S(2)}) %collective-permute-start.5) | collective-permute-done | bytes 81952 | tf_op jit(solution)/shard_map/ppermute | solution.py:151
  14.5 1.7 %collective-permute-start.6 = (bf16[80,512]{1,0:T(8,128)(2,1)S(1)}, bf16[80,512]{1,0:T(8,128)(2,1)S(1)}, u32[]{:S(2)}, u32[]{:S(2)}) collective-permute-start(bf16[80,512]{1,0:T(8,128)(2,1)S(1)} %collective-permute-done.5.refs_6_), channel_id=1, source_target_pairs={{0,4},{4,0},{8,12},{12,8},{16,20},{20,16},{24,28},{28,24},{1,5},{5... | collective-permute-start | bytes 245768 | tf_op jit(solution)/shard_map/ppermute | solution.py:151
  16.2 0.0 collective-permute-done.1.refs_2_
  16.2 0.4 %collective-permute-done.4.refs_5_ = bf16[80,512]{1,0:T(8,128)(2,1)S(1)} collective-permute-done((bf16[80,512]{1,0:T(8,128)(2,1)S(1)}, bf16[80,512]{1,0:T(8,128)(2,1)S(1)}, u32[]{:S(2)}, u32[]{:S(2)}) %collective-permute-start.4) | collective-permute-done | bytes 81952 | tf_op jit(solution)/shard_map/ppermute | solution.py:151
  16.6 0.3 collective-permute-done.2.refs_3_
  16.9 2.0 %collective-permute-done.6.refs_7_ = bf16[80,512]{1,0:T(8,128)(2,1)S(1)} collective-permute-done((bf16[80,512]{1,0:T(8,128)(2,1)S(1)}, bf16[80,512]{1,0:T(8,128)(2,1)S(1)}, u32[]{:S(2)}, u32[]{:S(2)}) %collective-permute-start.6) | collective-permute-done | bytes 81952 | tf_op jit(solution)/shard_map/ppermute | solution.py:151
  18.9 0.5 %shard_map.41 = (f32[2,80,160]{2,1,0:T(8,128)S(1)}, bf16[640,512]{1,0:T(8,128)(2,1)S(1)}) custom-call(bf16[88,512]{1,0:T(8,128)(2,1)S(1)} %pack.1.refs_0_, bf16[88,512]{1,0:T(8,128)(2,1)S(1)} %collective-permute-done.refs_1_, bf16[88,512]{1,0:T(8,128)(2,1)S(1)} %collective-permute-done.1.refs_2_, bf16[88,512]{1,0:T(8,128)(2,1)S(1)} %collective-permute-done.2.refs_3_, ...), custom_call_target="tpu_custom_call" | custom-call | tf_op jit(solution)/shard_map/pallas_call | solution.py:170
  19.5 0.1 collective-permute-start.7
  19.5 0.2 shard_map.42.kept_ref
  19.8 1.1 %collective-permute-done.7.got_ref = f32[2,80,160]{2,1,0:T(8,128)S(1)} collective-permute-done((f32[2,80,160]{2,1,0:T(8,128)S(1)}, f32[2,80,160]{2,1,0:T(8,128)S(1)}, u32[]{:S(2)}, u32[]{:S(2)}) %collective-permute-start.7) | collective-permute-done | bytes 102432 | tf_op jit(solution)/shard_map/ppermute | solution.py:151
  20.9 0.1 shard_map.43
  21.0 1.7 %collective-permute-start.8 = (bf16[104,128]{1,0:T(8,128)(2,1)S(1)}, bf16[104,128]{1,0:T(8,128)(2,1)S(1)}, u32[]{:S(2)}, u32[]{:S(2)}) collective-permute-start(bf16[104,128]{1,0:T(8,128)(2,1)S(1)} %get-tuple-element.9), channel_id=1, source_target_pairs={{0,2},{1,3},{2,0},{3,1},{4,6},{5,7},{6,4},{7,5},{8,10},{9,11},{10,... | collective-permute-start | bytes 79880 | tf_op jit(solution)/shard_map/ppermute | solution.py:151
  22.7 2.2 %collective-permute-start.9 = (bf16[32,128]{1,0:T(8,128)(2,1)S(1)}, bf16[32,128]{1,0:T(8,128)(2,1)S(1)}, u32[]{:S(2)}, u32[]{:S(2)}) collective-permute-start(bf16[32,128]{1,0:T(8,128)(2,1)S(1)} %shard_map.45.near_ref), channel_id=1, source_target_pairs={{0,16},{4,20},{8,24},{12,28},{16,0},{20,4},{24,8},{28,12},{1,17},{... | collective-permute-start | bytes 24584 | tf_op jit(solution)/shard_map/ppermute | solution.py:151
  24.8 2.4 %collective-permute-done.9.far_ref = bf16[32,128]{1,0:T(8,128)(2,1)S(1)} collective-permute-done((bf16[32,128]{1,0:T(8,128)(2,1)S(1)}, bf16[32,128]{1,0:T(8,128)(2,1)S(1)}, u32[]{:S(2)}, u32[]{:S(2)}) %collective-permute-start.9) | collective-permute-done | bytes 8224 | tf_op jit(solution)/shard_map/ppermute | solution.py:151
  27.2 0.8 %shard_map.46 = f32[1,512]{1,0:T(1,128)} custom-call(bf16[640,512]{1,0:T(8,128)(2,1)S(1)} %get-tuple-element.6.held_ref, bf16[32,128]{1,0:T(8,128)(2,1)S(1)} %shard_map.45.near_ref, bf16[32,128]{1,0:T(8,128)(2,1)S(1)} %collective-permute-done.9.far_ref), custom_call_target="tpu_custom_call" | custom-call | tf_op jit(solution)/shard_map/pallas_call | solution.py:176
  28.1 0.0 collective-permute-done.8.packed_ref
  28.1 0.7 %shard_map.44 = f32[80,160]{1,0:T(8,128)} custom-call(f32[80,160]{1,0:T(8,128)S(1)} %get-tuple-element.8.base_ref, bf16[104,128]{1,0:T(8,128)(2,1)S(1)} %collective-permute-done.8.packed_ref), custom_call_target="tpu_custom_call" | custom-call | tf_op jit(solution)/shard_map/pallas_call | solution.py:182
  (1 shorter events, 0.0 us)
Async XLA Ops:
  0.6 8.5 %collective-permute-start.3 = (bf16[80,512]{1,0:T(8,128)(2,1)}, bf16[80,512]{1,0:T(8,128)(2,1)S(1)}, u32[]{:S(2)}, u32[]{:S(2)}) collective-permute-start(bf16[80,512]{1,0:T(8,128)(2,1)} %values_hbm.1), channel_id=1, source_target_pairs={{0,16},{4,20},{8,24},{12,28},{16,0},{20,4},{24,8},{28,12},{1,17},{... | collective-permute-start | bytes 245768 | tf_op jit(solution)/shard_map/ppermute | solution.py:151
  5.7 5.5 %collective-permute-start = (bf16[88,512]{1,0:T(8,128)(2,1)S(1)}, bf16[88,512]{1,0:T(8,128)(2,1)S(1)}, u32[]{:S(2)}, u32[]{:S(2)}) collective-permute-start(bf16[88,512]{1,0:T(8,128)(2,1)S(1)} %pack.1.refs_0_), channel_id=1, source_target_pairs={{0,4},{4,0},{8,12},{12,8},{16,20},{20,16},{24,28},{28,24},{1,5},{5... | collective-permute-start | bytes 270344 | tf_op jit(solution)/shard_map/ppermute | solution.py:151
  9.2 5.3 %collective-permute-start.5 = (bf16[80,512]{1,0:T(8,128)(2,1)S(1)}, bf16[80,512]{1,0:T(8,128)(2,1)S(1)}, u32[]{:S(2)}, u32[]{:S(2)}) collective-permute-start(bf16[80,512]{1,0:T(8,128)(2,1)S(1)} %collective-permute-done.3.refs_4_), channel_id=1, source_target_pairs={{0,8},{4,12},{8,0},{12,4},{16,24},{20,28},{24,16},{28,20},{1,9},{5... | collective-permute-start | bytes 245768 | tf_op jit(solution)/shard_map/ppermute | solution.py:151
  10.0 6.2 %collective-permute-start.1 = (bf16[88,512]{1,0:T(8,128)(2,1)S(1)}, bf16[88,512]{1,0:T(8,128)(2,1)S(1)}, u32[]{:S(2)}, u32[]{:S(2)}) collective-permute-start(bf16[88,512]{1,0:T(8,128)(2,1)S(1)} %pack.1.refs_0_), channel_id=1, source_target_pairs={{0,8},{4,12},{8,0},{12,4},{16,24},{20,28},{24,16},{28,20},{1,9},{5... | collective-permute-start | bytes 270344 | tf_op jit(solution)/shard_map/ppermute | solution.py:151
  11.2 5.7 %collective-permute-start.2 = (bf16[88,512]{1,0:T(8,128)(2,1)S(1)}, bf16[88,512]{1,0:T(8,128)(2,1)S(1)}, u32[]{:S(2)}, u32[]{:S(2)}) collective-permute-start(bf16[88,512]{1,0:T(8,128)(2,1)S(1)} %collective-permute-done.refs_1_), channel_id=1, source_target_pairs={{0,8},{4,12},{8,0},{12,4},{16,24},{20,28},{24,16},{28,20},{1,9},{5... | collective-permute-start | bytes 270344 | tf_op jit(solution)/shard_map/ppermute | solution.py:151
  12.0 4.6 %collective-permute-start.4 = (bf16[80,512]{1,0:T(8,128)(2,1)S(1)}, bf16[80,512]{1,0:T(8,128)(2,1)S(1)}, u32[]{:S(2)}, u32[]{:S(2)}) collective-permute-start(bf16[80,512]{1,0:T(8,128)(2,1)S(1)} %collective-permute-done.3.refs_4_), channel_id=1, source_target_pairs={{0,4},{4,0},{8,12},{12,8},{16,20},{20,16},{24,28},{28,24},{1,5},{5... | collective-permute-start | bytes 245768 | tf_op jit(solution)/shard_map/ppermute | solution.py:151
  14.5 4.4 %collective-permute-start.6 = (bf16[80,512]{1,0:T(8,128)(2,1)S(1)}, bf16[80,512]{1,0:T(8,128)(2,1)S(1)}, u32[]{:S(2)}, u32[]{:S(2)}) collective-permute-start(bf16[80,512]{1,0:T(8,128)(2,1)S(1)} %collective-permute-done.5.refs_6_), channel_id=1, source_target_pairs={{0,4},{4,0},{8,12},{12,8},{16,20},{20,16},{24,28},{28,24},{1,5},{5... | collective-permute-start | bytes 245768 | tf_op jit(solution)/shard_map/ppermute | solution.py:151
  19.5 1.5 %collective-permute-start.7 = (f32[2,80,160]{2,1,0:T(8,128)S(1)}, f32[2,80,160]{2,1,0:T(8,128)S(1)}, u32[]{:S(2)}, u32[]{:S(2)}) collective-permute-start(f32[2,80,160]{2,1,0:T(8,128)S(1)} %get-tuple-element.7), channel_id=1, source_target_pairs={{0,1},{1,0},{2,3},{3,2},{4,5},{5,4},{6,7},{7,6},{8,9},{9,8},{10,11... | collective-permute-start | bytes 307208 | tf_op jit(solution)/shard_map/ppermute | solution.py:151
  21.0 7.1 %collective-permute-start.8 = (bf16[104,128]{1,0:T(8,128)(2,1)S(1)}, bf16[104,128]{1,0:T(8,128)(2,1)S(1)}, u32[]{:S(2)}, u32[]{:S(2)}) collective-permute-start(bf16[104,128]{1,0:T(8,128)(2,1)S(1)} %get-tuple-element.9), channel_id=1, source_target_pairs={{0,2},{1,3},{2,0},{3,1},{4,6},{5,7},{6,4},{7,5},{8,10},{9,11},{10,... | collective-permute-start | bytes 79880 | tf_op jit(solution)/shard_map/ppermute | solution.py:151
  22.7 4.5 %collective-permute-start.9 = (bf16[32,128]{1,0:T(8,128)(2,1)S(1)}, bf16[32,128]{1,0:T(8,128)(2,1)S(1)}, u32[]{:S(2)}, u32[]{:S(2)}) collective-permute-start(bf16[32,128]{1,0:T(8,128)(2,1)S(1)} %shard_map.45.near_ref), channel_id=1, source_target_pairs={{0,16},{4,20},{8,24},{12,28},{16,0},{20,4},{24,8},{28,12},{1,17},{... | collective-permute-start | bytes 24584 | tf_op jit(solution)/shard_map/ppermute | solution.py:151

commit v6 on v5

--- a/solution.py
+++ b/solution.py
@@ -71,9 +71,11 @@
 
 
 def tails_kernel(*refs):
-    for slot, ref in enumerate(refs[:-1]):
-        tail = ref[ref.shape[0] - EXTRA :, : refs[-1].shape[1]]
-        refs[-1][slot * EXTRA : (slot + 1) * EXTRA, :] = tail
+    packed, raw, (tails_ref, sums_ref) = refs[:4], refs[4:-2], refs[-2:]
+    for slot, ref in enumerate(packed):
+        tails_ref[slot * EXTRA : (slot + 1) * EXTRA, :] = ref[ref.shape[0] - EXTRA :, : tails_ref.shape[1]]
+    for slot, ref in enumerate(raw):
+        sums_ref[slot : slot + 1, :] = jnp.sum(ref[...].astype(jnp.float32), axis=0, keepdims=True)
 
 
 def source_of(step):
@@ -91,13 +93,15 @@
     return lax.dot_general(left, right, (((1,), (1,)), ((), ())), preferred_element_type=jnp.float32)
 
 
-def send_kernel(total_rows, *refs):
+def send_kernel(total_rows, early, sums_ref, *refs):
     blocks, (sent_ref, held_ref, lines) = refs[:-3], refs[-3:]
     rows = total_rows // len(blocks)
     factor = 1.0 / math.sqrt(total_rows)
     for step, block in enumerate(blocks):
         if block.shape[0] > rows:
             line = jnp.sum(block[rows:, :].astype(jnp.float32)[PARTS : 2 * PARTS, :], axis=0, keepdims=True)
+        elif step in early:
+            line = sums_ref[early.index(step) : early.index(step) + 1, :]
         else:
             line = jnp.sum(block[...].astype(jnp.float32), axis=0, keepdims=True)
         lines[pl.ds(source_of(step), 1), :] = line
@@ -163,13 +167,16 @@
     far_other = swap(far, "smp", 1)
     far_beside_other = swap(far_beside, "smp", 1)
     near = (own, other, beside, beside_other)
-    tails = call(tails_kernel, jax.ShapeDtypeStruct((len(near) * EXTRA, LANES), jnp.bfloat16))(*near)
+    shapes = (jax.ShapeDtypeStruct((len(near) * EXTRA, LANES), jnp.bfloat16), jax.ShapeDtypeStruct((2, columns), jnp.float32))
+    tails, early_sums = call(tails_kernel, shapes)(*near, far, far_beside)
     far_tails = swap(tails, "smp", 4)
     tile = jax.ShapeDtypeStruct((2, rows, rows * n // m), jnp.float32)
     lines = [pltpu.VMEM((n + SPARE, columns), jnp.float32)]
     sent, held = call(
-        functools.partial(send_kernel, rows * n), (tile, jax.ShapeDtypeStruct((n * rows, columns), jnp.bfloat16)), lines
-    )(*near, far, far_other, far_beside, far_beside_other)
+        functools.partial(send_kernel, rows * n, (4, 6)),
+        (tile, jax.ShapeDtypeStruct((n * rows, columns), jnp.bfloat16)),
+        lines,
+    )(early_sums, *near, far, far_other, far_beside, far_beside_other)
     got = swap(sent, "par", 1)
     kept = call(functools.partial(keep_kernel, rows), tile)(held)
     line = jax.ShapeDtypeStruct((1, columns), jnp.float32)

time: 28.9 us -> 28.9 us (level)
  transfers between devices with their start and end apart: 10 -> 10, of which waited for: 7 -> 6; matrix products, arithmetic and copies ran while one was open for 0% -> 0% of each run, Pallas kernels for 7% -> 7%
where the time goes in v6:
time: 28.9 us; the launch traced here: 28.8 us
  starting transfers between devices  15.7 us (54%)
  waiting for transfers between devices  9.02 us (31%)
  Pallas kernels  3.36 us (12%)
  between operations  0.67 us (2%)
    ppermute x10, starting transfers between devices, swap(): lax.ppermute(value, axis, [(i, i ^ bit) for i in range(lax.axis_size(axis...  15.7 us
    ppermute x10, waiting for transfers between devices, swap(): lax.ppermute(value, axis, [(i, i ^ bit) for i in range(lax.axis_size(axis...  9.02 us
    pallas_call x1, Pallas kernels, pack(): pl.pallas_call(pack_kernel, out_shape=jax.ShapeDtypeStruct((rows + EXTRA,...  0.97 us
    pallas_call x1, Pallas kernels, direct(): call(functools.partial(update_kernel, rows), line, lines)  0.82 us
    pallas_call x1, Pallas kernels, direct(): call(last_kernel, jax.ShapeDtypeStruct(tile.shape[1:], jnp.float32))  0.71 us
  transfers between devices with their start and end apart: 10, of which 6 were waited for; matrix products, arithmetic and copies ran while one was open for 0% of the time, Pallas kernels for 7%

profile of v6, /device:TPU:0, one launch (start us, length us, event | category | flops | bytes accessed | tf_op | source)
XLA Modules:
  0.0 28.8 jit_solution(7944901403704720491)
XLA Ops:
  0.6 4.1 %collective-permute-start.3 = (bf16[80,512]{1,0:T(8,128)(2,1)}, bf16[80,512]{1,0:T(8,128)(2,1)S(1)}, u32[]{:S(2)}, u32[]{:S(2)}) collective-permute-start(bf16[80,512]{1,0:T(8,128)(2,1)} %values_hbm.1), channel_id=1, source_target_pairs={{0,16},{4,20},{8,24},{12,28},{16,0},{20,4},{24,8},{28,12},{1,17},{... | collective-permute-start | bytes 245768 | tf_op jit(solution)/shard_map/ppermute | solution.py:155
  4.8 1.0 %pack.1.refs_0_ = bf16[88,512]{1,0:T(8,128)(2,1)S(1)} custom-call(bf16[80,512]{1,0:T(8,128)(2,1)} %values_hbm.1, f32[1,80]{1,0:T(1,128)} %bitcast.3), custom_call_target="tpu_custom_call" | custom-call | tf_op jit(solution)/shard_map/pack/pallas_call | solution.py:63
  5.7 1.6 %collective-permute-start = (bf16[88,512]{1,0:T(8,128)(2,1)S(1)}, bf16[88,512]{1,0:T(8,128)(2,1)S(1)}, u32[]{:S(2)}, u32[]{:S(2)}) collective-permute-start(bf16[88,512]{1,0:T(8,128)(2,1)S(1)} %pack.1.refs_0_), channel_id=1, source_target_pairs={{0,4},{4,0},{8,12},{12,8},{16,20},{20,16},{24,28},{28,24},{1,5},{5... | collective-permute-start | bytes 270344 | tf_op jit(solution)/shard_map/ppermute | solution.py:155
  7.3 1.9 %collective-permute-done.3.refs_4_ = bf16[80,512]{1,0:T(8,128)(2,1)S(1)} collective-permute-done((bf16[80,512]{1,0:T(8,128)(2,1)}, bf16[80,512]{1,0:T(8,128)(2,1)S(1)}, u32[]{:S(2)}, u32[]{:S(2)}) %collective-permute-start.3) | collective-permute-done | bytes 81952 | tf_op jit(solution)/shard_map/ppermute | solution.py:155
  9.2 0.8 %collective-permute-start.4 = (bf16[80,512]{1,0:T(8,128)(2,1)S(1)}, bf16[80,512]{1,0:T(8,128)(2,1)S(1)}, u32[]{:S(2)}, u32[]{:S(2)}) collective-permute-start(bf16[80,512]{1,0:T(8,128)(2,1)S(1)} %collective-permute-done.3.refs_4_), channel_id=1, source_target_pairs={{0,8},{4,12},{8,0},{12,4},{16,24},{20,28},{24,16},{28,20},{1,9},{5... | collective-permute-start | bytes 245768 | tf_op jit(solution)/shard_map/ppermute | solution.py:155
  10.0 1.2 %collective-permute-start.1 = (bf16[88,512]{1,0:T(8,128)(2,1)S(1)}, bf16[88,512]{1,0:T(8,128)(2,1)S(1)}, u32[]{:S(2)}, u32[]{:S(2)}) collective-permute-start(bf16[88,512]{1,0:T(8,128)(2,1)S(1)} %pack.1.refs_0_), channel_id=1, source_target_pairs={{0,8},{4,12},{8,0},{12,4},{16,24},{20,28},{24,16},{28,20},{1,9},{5... | collective-permute-start | bytes 270344 | tf_op jit(solution)/shard_map/ppermute | solution.py:155
  11.2 0.0 collective-permute-done.refs_1_
  11.2 0.8 %collective-permute-start.2 = (bf16[88,512]{1,0:T(8,128)(2,1)S(1)}, bf16[88,512]{1,0:T(8,128)(2,1)S(1)}, u32[]{:S(2)}, u32[]{:S(2)}) collective-permute-start(bf16[88,512]{1,0:T(8,128)(2,1)S(1)} %collective-permute-done.refs_1_), channel_id=1, source_target_pairs={{0,8},{4,12},{8,0},{12,4},{16,24},{20,28},{24,16},{28,20},{1,9},{5... | collective-permute-start | bytes 270344 | tf_op jit(solution)/shard_map/ppermute | solution.py:155
  12.0 1.5 %collective-permute-start.5 = (bf16[80,512]{1,0:T(8,128)(2,1)S(1)}, bf16[80,512]{1,0:T(8,128)(2,1)S(1)}, u32[]{:S(2)}, u32[]{:S(2)}) collective-permute-start(bf16[80,512]{1,0:T(8,128)(2,1)S(1)} %collective-permute-done.3.refs_4_), channel_id=1, source_target_pairs={{0,4},{4,0},{8,12},{12,8},{16,20},{20,16},{24,28},{28,24},{1,5},{5... | collective-permute-start | bytes 245768 | tf_op jit(solution)/shard_map/ppermute | solution.py:155
  13.5 0.9 %collective-permute-done.4.refs_5_.refs_6_ = bf16[80,512]{1,0:T(8,128)(2,1)S(1)} collective-permute-done((bf16[80,512]{1,0:T(8,128)(2,1)S(1)}, bf16[80,512]{1,0:T(8,128)(2,1)S(1)}, u32[]{:S(2)}, u32[]{:S(2)}) %collective-permute-start.4) | collective-permute-done | bytes 81952 | tf_op jit(solution)/shard_map/ppermute | solution.py:155
  14.5 1.7 %collective-permute-start.6 = (bf16[80,512]{1,0:T(8,128)(2,1)S(1)}, bf16[80,512]{1,0:T(8,128)(2,1)S(1)}, u32[]{:S(2)}, u32[]{:S(2)}) collective-permute-start(bf16[80,512]{1,0:T(8,128)(2,1)S(1)} %collective-permute-done.4.refs_5_.refs_6_), channel_id=1, source_target_pairs={{0,4},{4,0},{8,12},{12,8},{16,20},{20,16},{24,28},{28,24},{1,5},{5... | collective-permute-start | bytes 245768 | tf_op jit(solution)/shard_map/ppermute | solution.py:155
  16.2 0.0 collective-permute-done.1.refs_2_
  16.2 0.7 %collective-permute-done.2.refs_3_ = bf16[88,512]{1,0:T(8,128)(2,1)S(1)} collective-permute-done((bf16[88,512]{1,0:T(8,128)(2,1)S(1)}, bf16[88,512]{1,0:T(8,128)(2,1)S(1)}, u32[]{:S(2)}, u32[]{:S(2)}) %collective-permute-start.2) | collective-permute-done | bytes 90144 | tf_op jit(solution)/shard_map/ppermute | solution.py:155
  17.0 0.0 collective-permute-done.5.refs_5_
  17.0 2.0 %collective-permute-done.6.refs_7_ = bf16[80,512]{1,0:T(8,128)(2,1)S(1)} collective-permute-done((bf16[80,512]{1,0:T(8,128)(2,1)S(1)}, bf16[80,512]{1,0:T(8,128)(2,1)S(1)}, u32[]{:S(2)}, u32[]{:S(2)}) %collective-permute-start.6) | collective-permute-done | bytes 81952 | tf_op jit(solution)/shard_map/ppermute | solution.py:155
  18.9 0.5 %shard_map.42 = (f32[2,80,160]{2,1,0:T(8,128)S(1)}, bf16[640,512]{1,0:T(8,128)(2,1)S(1)}) custom-call(f32[2,512]{1,0:T(2,128)S(1)} %get-tuple-element.8.sums_ref, bf16[88,512]{1,0:T(8,128)(2,1)S(1)} %pack.1.refs_0_, bf16[88,512]{1,0:T(8,128)(2,1)S(1)} %collective-permute-done.refs_1_, bf16[88,512]{1,0:T(8,128)(2,1)S(1)} %collective-permute-done.1.refs_2_, ...), custom_call_target="tpu_custom_call" | custom-call | tf_op jit(solution)/shard_map/pallas_call | solution.py:175
  19.4 0.1 collective-permute-start.7
  19.5 0.2 shard_map.43.kept_ref
  19.7 1.1 %collective-permute-done.7.got_ref = f32[2,80,160]{2,1,0:T(8,128)S(1)} collective-permute-done((f32[2,80,160]{2,1,0:T(8,128)S(1)}, f32[2,80,160]{2,1,0:T(8,128)S(1)}, u32[]{:S(2)}, u32[]{:S(2)}) %collective-permute-start.7) | collective-permute-done | bytes 102432 | tf_op jit(solution)/shard_map/ppermute | solution.py:155
  20.9 0.1 shard_map.44
  21.0 1.7 %collective-permute-start.8 = (bf16[104,128]{1,0:T(8,128)(2,1)S(1)}, bf16[104,128]{1,0:T(8,128)(2,1)S(1)}, u32[]{:S(2)}, u32[]{:S(2)}) collective-permute-start(bf16[104,128]{1,0:T(8,128)(2,1)S(1)} %get-tuple-element.12), channel_id=1, source_target_pairs={{0,2},{1,3},{2,0},{3,1},{4,6},{5,7},{6,4},{7,5},{8,10},{9,11},{10,... | collective-permute-start | bytes 79880 | tf_op jit(solution)/shard_map/ppermute | solution.py:155
  22.7 2.2 %collective-permute-start.9 = (bf16[32,128]{1,0:T(8,128)(2,1)S(1)}, bf16[32,128]{1,0:T(8,128)(2,1)S(1)}, u32[]{:S(2)}, u32[]{:S(2)}) collective-permute-start(bf16[32,128]{1,0:T(8,128)(2,1)S(1)} %get-tuple-element.13.near_ref), channel_id=1, source_target_pairs={{0,16},{4,20},{8,24},{12,28},{16,0},{20,4},{24,8},{28,12},{1,17},{... | collective-permute-start | bytes 24584 | tf_op jit(solution)/shard_map/ppermute | solution.py:155
  24.8 2.4 %collective-permute-done.9.far_ref = bf16[32,128]{1,0:T(8,128)(2,1)S(1)} collective-permute-done((bf16[32,128]{1,0:T(8,128)(2,1)S(1)}, bf16[32,128]{1,0:T(8,128)(2,1)S(1)}, u32[]{:S(2)}, u32[]{:S(2)}) %collective-permute-start.9) | collective-permute-done | bytes 8224 | tf_op jit(solution)/shard_map/ppermute | solution.py:155
  27.2 0.8 %shard_map.46 = f32[1,512]{1,0:T(1,128)} custom-call(bf16[640,512]{1,0:T(8,128)(2,1)S(1)} %get-tuple-element.9.held_ref, bf16[32,128]{1,0:T(8,128)(2,1)S(1)} %get-tuple-element.13.near_ref, bf16[32,128]{1,0:T(8,128)(2,1)S(1)} %collective-permute-done.9.far_ref), custom_call_target="tpu_custom_call" | custom-call | tf_op jit(solution)/shard_map/pallas_call | solution.py:183
  28.0 0.0 collective-permute-done.8.packed_ref
  28.0 0.7 %shard_map.45 = f32[80,160]{1,0:T(8,128)} custom-call(f32[80,160]{1,0:T(8,128)S(1)} %get-tuple-element.11.base_ref, bf16[104,128]{1,0:T(8,128)(2,1)S(1)} %collective-permute-done.8.packed_ref), custom_call_target="tpu_custom_call" | custom-call | tf_op jit(solution)/shard_map/pallas_call | solution.py:189
  (1 shorter events, 0.0 us)
Async XLA Ops:
  0.6 8.5 %collective-permute-start.3 = (bf16[80,512]{1,0:T(8,128)(2,1)}, bf16[80,512]{1,0:T(8,128)(2,1)S(1)}, u32[]{:S(2)}, u32[]{:S(2)}) collective-permute-start(bf16[80,512]{1,0:T(8,128)(2,1)} %values_hbm.1), channel_id=1, source_target_pairs={{0,16},{4,20},{8,24},{12,28},{16,0},{20,4},{24,8},{28,12},{1,17},{... | collective-permute-start | bytes 245768 | tf_op jit(solution)/shard_map/ppermute | solution.py:155
  5.7 5.5 %collective-permute-start = (bf16[88,512]{1,0:T(8,128)(2,1)S(1)}, bf16[88,512]{1,0:T(8,128)(2,1)S(1)}, u32[]{:S(2)}, u32[]{:S(2)}) collective-permute-start(bf16[88,512]{1,0:T(8,128)(2,1)S(1)} %pack.1.refs_0_), channel_id=1, source_target_pairs={{0,4},{4,0},{8,12},{12,8},{16,20},{20,16},{24,28},{28,24},{1,5},{5... | collective-permute-start | bytes 270344 | tf_op jit(solution)/shard_map/ppermute | solution.py:155
  9.2 5.3 %collective-permute-start.4 = (bf16[80,512]{1,0:T(8,128)(2,1)S(1)}, bf16[80,512]{1,0:T(8,128)(2,1)S(1)}, u32[]{:S(2)}, u32[]{:S(2)}) collective-permute-start(bf16[80,512]{1,0:T(8,128)(2,1)S(1)} %collective-permute-done.3.refs_4_), channel_id=1, source_target_pairs={{0,8},{4,12},{8,0},{12,4},{16,24},{20,28},{24,16},{28,20},{1,9},{5... | collective-permute-start | bytes 245768 | tf_op jit(solution)/shard_map/ppermute | solution.py:155
  10.0 6.2 %collective-permute-start.1 = (bf16[88,512]{1,0:T(8,128)(2,1)S(1)}, bf16[88,512]{1,0:T(8,128)(2,1)S(1)}, u32[]{:S(2)}, u32[]{:S(2)}) collective-permute-start(bf16[88,512]{1,0:T(8,128)(2,1)S(1)} %pack.1.refs_0_), channel_id=1, source_target_pairs={{0,8},{4,12},{8,0},{12,4},{16,24},{20,28},{24,16},{28,20},{1,9},{5... | collective-permute-start | bytes 270344 | tf_op jit(solution)/shard_map/ppermute | solution.py:155
  11.2 5.7 %collective-permute-start.2 = (bf16[88,512]{1,0:T(8,128)(2,1)S(1)}, bf16[88,512]{1,0:T(8,128)(2,1)S(1)}, u32[]{:S(2)}, u32[]{:S(2)}) collective-permute-start(bf16[88,512]{1,0:T(8,128)(2,1)S(1)} %collective-permute-done.refs_1_), channel_id=1, source_target_pairs={{0,8},{4,12},{8,0},{12,4},{16,24},{20,28},{24,16},{28,20},{1,9},{5... | collective-permute-start | bytes 270344 | tf_op jit(solution)/shard_map/ppermute | solution.py:155
  12.0 4.9 %collective-permute-start.5 = (bf16[80,512]{1,0:T(8,128)(2,1)S(1)}, bf16[80,512]{1,0:T(8,128)(2,1)S(1)}, u32[]{:S(2)}, u32[]{:S(2)}) collective-permute-start(bf16[80,512]{1,0:T(8,128)(2,1)S(1)} %collective-permute-done.3.refs_4_), channel_id=1, source_target_pairs={{0,4},{4,0},{8,12},{12,8},{16,20},{20,16},{24,28},{28,24},{1,5},{5... | collective-permute-start | bytes 245768 | tf_op jit(solution)/shard_map/ppermute | solution.py:155
  14.5 4.4 %collective-permute-start.6 = (bf16[80,512]{1,0:T(8,128)(2,1)S(1)}, bf16[80,512]{1,0:T(8,128)(2,1)S(1)}, u32[]{:S(2)}, u32[]{:S(2)}) collective-permute-start(bf16[80,512]{1,0:T(8,128)(2,1)S(1)} %collective-permute-done.4.refs_5_.refs_6_), channel_id=1, source_target_pairs={{0,4},{4,0},{8,12},{12,8},{16,20},{20,16},{24,28},{28,24},{1,5},{5... | collective-permute-start | bytes 245768 | tf_op jit(solution)/shard_map/ppermute | solution.py:155
  19.4 1.5 %collective-permute-start.7 = (f32[2,80,160]{2,1,0:T(8,128)S(1)}, f32[2,80,160]{2,1,0:T(8,128)S(1)}, u32[]{:S(2)}, u32[]{:S(2)}) collective-permute-start(f32[2,80,160]{2,1,0:T(8,128)S(1)} %get-tuple-element.10), channel_id=1, source_target_pairs={{0,1},{1,0},{2,3},{3,2},{4,5},{5,4},{6,7},{7,6},{8,9},{9,8},{10,11... | collective-permute-start | bytes 307208 | tf_op jit(solution)/shard_map/ppermute | solution.py:155
  21.0 7.1 %collective-permute-start.8 = (bf16[104,128]{1,0:T(8,128)(2,1)S(1)}, bf16[104,128]{1,0:T(8,128)(2,1)S(1)}, u32[]{:S(2)}, u32[]{:S(2)}) collective-permute-start(bf16[104,128]{1,0:T(8,128)(2,1)S(1)} %get-tuple-element.12), channel_id=1, source_target_pairs={{0,2},{1,3},{2,0},{3,1},{4,6},{5,7},{6,4},{7,5},{8,10},{9,11},{10,... | collective-permute-start | bytes 79880 | tf_op jit(solution)/shard_map/ppermute | solution.py:155
  22.7 4.5 %collective-permute-start.9 = (bf16[32,128]{1,0:T(8,128)(2,1)S(1)}, bf16[32,128]{1,0:T(8,128)(2,1)S(1)}, u32[]{:S(2)}, u32[]{:S(2)}) collective-permute-start(bf16[32,128]{1,0:T(8,128)(2,1)S(1)} %get-tuple-element.13.near_ref), channel_id=1, source_target_pairs={{0,16},{4,20},{8,24},{12,28},{16,0},{20,4},{24,8},{28,12},{1,17},{... | collective-permute-start | bytes 24584 | tf_op jit(solution)/shard_map/ppermute | solution.py:155
